TPU v7x, 512 devices: a whole 4x8x8 slice. The times are simulated.
512 devices in a mesh: row: 16 (over y, core), col: 32 (over x, z).
Axes of the slice: x: 4, y: 8, z: 8, core: 2. Of those that a mesh axis runs over, the one named last changes fastest.
Arguments:
- operator_blocks: float32 [4096, 64, 512], P(('row', 'col')), may hold values from -0.75 to 0.75
- operator_count: int32 [4096], P(('row', 'col')), may hold values from 1 to 8
- operator_slot: int32 [4096, 8], P(('row', 'col')), may hold values from 0 to 127
- fetch_lists: int32 [16, 32, 32, 4], P('row', 'col'), may hold values from 0 to 4095, as said below
- prolong_blocks: float32 [4096, 64, 128], P(('row', 'col')), may hold values from -0.75 to 0.75
- prolong_cols: int32 [4096, 2], P(('row', 'col')), may hold values from 0 to 31
- restrict_blocks: float32 [4096, 64, 128], P(('row', 'col')), may hold values from -0.09375 to 0.09375
- restrict_rows: int32 [4096, 2], P(('row', 'col')), may hold values from 0 to 1
Outputs:
- coarse_operator: float32 [2048, 2048], P('row', 'col')
Inputs may be any that keep to these rules, and one draw needn't show every extreme that they name: fetch_lists[r, c, p, s] names a fine block held by the device with column index p and row index r2 = (r + c + p * 4 + s + h) mod 16, for one whole number h of the draw; that device holds fine blocks (r2 * 32 + p) * 8 to (r2 * 32 + p + 1) * 8 - 1.
All inputs are finite; a program needn't handle non-finite values.
Results may differ from a plain program's by a relative error of at most 0.0003.
Values sent between devices are 32-bit elements; how exact they have to be, the bound alone decides.
A program may use at most 64 MiB of HBM per device.

v0:
```python
import jax
import jax.numpy as jnp
from jax import lax
from jax.sharding import PartitionSpec as P

NCR = 2


def contract(form, left, right):
    return jnp.einsum(form, left, right, precision=lax.Precision.HIGHEST)


def gather_panel(prolong_blocks, prolong_cols):
    return (
        lax.all_gather(prolong_blocks, "row", axis=0, tiled=True),
        lax.all_gather(prolong_cols, "row", axis=0, tiled=True),
    )


def local(
    operator_blocks,
    operator_count,
    operator_slot,
    fetch_lists,
    prolong_blocks,
    prolong_cols,
    restrict_blocks,
    restrict_rows,
):
    fine_rows = operator_blocks.shape[0]
    block_size = operator_blocks.shape[1]
    row_entries = operator_slot.shape[1]
    prolong_entries = prolong_cols.shape[1]
    restrict_entries = restrict_rows.shape[1]
    columns = lax.axis_size("col")
    slot_count = fetch_lists.shape[3]
    total_slots = columns * slot_count
    coarse_all = NCR * lax.axis_size("row")
    live_mask = (
        jnp.arange(row_entries, dtype=jnp.int32)[None, :] < operator_count[:, None]
    ).astype(jnp.float32)
    blocks = operator_blocks.reshape(fine_rows, block_size, row_entries, block_size)
    restrict_hot = (restrict_rows[..., None] == jnp.arange(NCR, dtype=jnp.int32)).astype(
        jnp.float32
    )
    restrict_dense = contract(
        "iaqb,iqQ->iaQb",
        restrict_blocks.reshape(fine_rows, block_size, restrict_entries, block_size),
        restrict_hot,
    )
    requests = fetch_lists.reshape(columns, slot_count)
    panel_blocks, panel_columns = gather_panel(prolong_blocks, prolong_cols)
    wanted = lax.all_to_all(requests, "col", split_axis=0, concat_axis=0, tiled=True)
    position = wanted // (fine_rows * columns) * fine_rows + wanted % fine_rows
    fetched = panel_blocks[position]
    fetched_columns = panel_columns[position]
    got_blocks = lax.all_to_all(fetched, "col", split_axis=0, concat_axis=0, tiled=True)
    got_columns = lax.all_to_all(fetched_columns, "col", split_axis=0, concat_axis=0, tiled=True)
    got_blocks = got_blocks.reshape(total_slots, block_size, prolong_entries * block_size)
    got_columns = got_columns.reshape(total_slots, prolong_entries)
    picked = got_blocks[operator_slot]
    picked_columns = got_columns[operator_slot]
    products = contract("iakb,ikbn->ikan", blocks, picked)
    prolong_hot = (picked_columns[..., None] == jnp.arange(coarse_all, dtype=jnp.int32)).astype(
        jnp.float32
    ) * live_mask[:, :, None, None]
    product_dense = contract(
        "ikamc,ikmJ->iaJc",
        products.reshape(fine_rows, row_entries, block_size, prolong_entries, block_size),
        prolong_hot,
    )
    partial_value = contract("iaQb,iaJc->QbJc", restrict_dense, product_dense)
    partial_value = partial_value.reshape(NCR * block_size, coarse_all * block_size)
    return lax.psum_scatter(partial_value, "col", scatter_dimension=1, tiled=True)


def solution(mesh):
    return jax.shard_map(
        local,
        mesh=mesh,
        in_specs=(
            P(("row", "col"), None, None),
            P(("row", "col")),
            P(("row", "col"), None),
            P("row", "col", None, None),
            P(("row", "col"), None, None),
            P(("row", "col"), None),
            P(("row", "col"), None, None),
            P(("row", "col"), None),
        ),
        out_specs=P("row", "col"),
        check_vma=False,
    )
```

profile of v0, /device:TPU:1, one launch (start us, length us, event | category | flops | bytes accessed | tf_op | source)
XLA Modules:
  0.0 428.1 jit_solution(5289201583675393657)
XLA Ops:
  6.5 0.7 all-gather.3.cloned.1.call-update
  7.3 1.4 copy.25
  8.6 13.7 %all-to-all-start = ((s32[32,1,4]{2,1,0:T(1,128)}), s32[32,1,4]{2,1,0:T(1,128)S(1)}, u32[]{:S(2)}, u32[]{:S(2)}) async-start(s32[32,1,4]{2,1,0:T(1,128)} %copy.25), calls=%async_computation | async-start | bytes 32768 | tf_op jit(solution)/shard_map/all_to_all | solution.py:53
  22.3 18.6 %all-gather = s32[16,8,2]{1,2,0:T(2,128)S(1)} all-gather(s32[1,8,2]{1,2,0:T(2,128)} %bitcast.74), channel_id=1, replica_groups=mesh['row'=16,'col'=32] {'row'}, dimensions={0}, use_global_device_ids=true | all-gather | bytes 1088 | tf_op jit(solution)/shard_map/all_gather | solution.py:16
  41.4 0.6 gather_fusion
  42.1 0.9 copy.28
  43.0 9.5 %all-to-all-start.1 = ((s32[32,4,2]{1,2,0:T(2,128)}), s32[32,4,2]{1,2,0:T(2,128)S(1)}, u32[]{:S(2)}, u32[]{:S(2)}) async-start(s32[32,4,2]{1,2,0:T(2,128)} %copy.28), calls=%async_computation.1 | async-start | bytes 65536 | tf_op jit(solution)/shard_map/all_to_all | solution.py:58
  52.5 7.5 %all-gather.3.cloned.1.call-done = f32[128,64,128]{2,1,0:T(8,128)} async-done(((f32[8,64,128]{2,1,0:T(8,128)}), f32[128,64,128]{2,1,0:T(8,128)}) %all-gather.3.cloned.1.call-update) | async-done | bytes 4194320 | tf_op jit(solution)/shard_map/all_gather | solution.py:15
  60.0 4.9 %gather_fusion.2 = f32[128,64,128]{2,1,0:T(8,128)} fusion(f32[128,64,128]{2,1,0:T(8,128)} %all-gather.3.cloned.1.call-done, s32[1024]{0:T(1024)S(1)} %pad_clamp_fusion.1), kind=kCustom, calls=%fused_computation.2 | custom fusion | bytes 8389120 | tf_op jit(solution)/shard_map/gather | solution.py:55
  65.0 10.4 %all-to-all-start.2 = ((f32[32,4,64,128]{3,2,1,0:T(8,128)}), f32[32,4,64,128]{3,2,1,0:T(8,128)}, u32[]{:S(2)}, u32[]{:S(2)}) async-start(f32[32,4,64,128]{3,2,1,0:T(8,128)} %bitcast.66), calls=%async_computation.2 | async-start | bytes 8388608 | tf_op jit(solution)/shard_map/all_to_all | solution.py:57
  75.7 1.8 reshape.167
  77.5 0.3 reshape.164
  78.0 1.1 convolution_bitcast_fusion
  79.1 0.3 copy.29
  79.5 0.6 gather_fusion.1
  80.2 89.6 %all-to-all-done.2 = f32[32,4,64,128]{3,2,1,0:T(8,128)} async-done(((f32[32,4,64,128]{3,2,1,0:T(8,128)}), f32[32,4,64,128]{3,2,1,0:T(8,128)}, u32[]{:S(2)}, u32[]{:S(2)}) %all-to-all-start.2) | async-done | bytes 4194336 | tf_op jit(solution)/shard_map/all_to_all | solution.py:57
  169.7 2.9 gather_fusion.3
  172.6 5.2 %fusion.13 = f32[8,8,64,128]{3,2,1,0:T(8,128)} fusion(f32[8,8,64,128]{3,2,1,0:T(8,128)S(1)} %bitcast.67, f32[8,64,8,64]{3,2,1,0:T(8,128)} %reshape.167), kind=kOutput, calls=%fused_computation.13 | convolution fusion | flops 402653184 | bytes 5242880 | tf_op jit(solution)/shard_map/iakb,ikbn->ikan/dot_general | solution.py:10
  177.8 5.6 %reshape.168 = f32[8,8,64,2,64]{4,3,2,1,0:T(2,128)} reshape(f32[8,8,64,128]{3,2,1,0:T(8,128)} %fusion.13) | data formatting | bytes 4194304 | tf_op jit(solution)/shard_map/reshape | solution.py:69
  183.4 11.2 %fusion.5 = f32[8,64,32,64]{3,2,1,0:T(8,128)S(1)} fusion(f32[8,8,64,2,64]{4,3,2,1,0:T(2,128)} %reshape.168, f32[8,8]{1,0:T(8,128)S(1)} %fusion.26, s32[8,8,2]{1,2,0:T(2,128)S(1)} %copy.31), kind=kOutput, calls=%fused_computation.9 | convolution fusion | flops 201334784 | bytes 6292224 | tf_op jit(solution)/shard_map/ikamc,ikmJ->iaJc/dot_general | solution.py:10
  194.6 9.3 %fusion.10 = f32[2,64,32,64]{3,1,2,0:T(8,128)S(1)} fusion(f32[8,64,32,64]{3,2,1,0:T(8,128)S(1)} %fusion.5, f32[8,64,2,64,1]{3,2,1,0,4:T(2,128)S(1)} %convolution_bitcast_fusion), kind=kOutput, calls=%fused_computation.12 | convolution fusion | flops 1610612736 | bytes 5505024 | tf_op jit(solution)/shard_map/iaQb,iaJc->QbJc/dot_general | solution.py:10
  203.9 2.3 copy.49
  206.3 3.3 reshape.218
  209.7 211.6 %reduce-scatter.4.cloned.1.call-done = f32[64,128]{1,0:T(8,128)} async-done(((f32[2048,128]{1,0:T(8,128)}), f32[64,128]{1,0:T(8,128)}) %reduce-scatter.4.cloned.1.call-update) | async-done | bytes 32784
  (27 shorter events, 1.1 us)
Async XLA Ops:
  6.5 53.5 %all-gather.3.cloned.1.call-start = ((), (), s32[]{:S(2)}) async-start(), calls=%async_computation.4 | async-start | bytes 4456448 | tf_op jit(solution)/shard_map/all_gather | solution.py:15
  8.6 32.5 %all-to-all-start = ((s32[32,1,4]{2,1,0:T(1,128)}), s32[32,1,4]{2,1,0:T(1,128)S(1)}, u32[]{:S(2)}, u32[]{:S(2)}) async-start(s32[32,1,4]{2,1,0:T(1,128)} %copy.25), calls=%async_computation | async-start | bytes 32768 | tf_op jit(solution)/shard_map/all_to_all | solution.py:53
  43.0 21.9 %all-to-all-start.1 = ((s32[32,4,2]{1,2,0:T(2,128)}), s32[32,4,2]{1,2,0:T(2,128)S(1)}, u32[]{:S(2)}, u32[]{:S(2)}) async-start(s32[32,4,2]{1,2,0:T(2,128)} %copy.28), calls=%async_computation.1 | async-start | bytes 65536 | tf_op jit(solution)/shard_map/all_to_all | solution.py:58
  64.9 10.7 %copy-start.2 = (s32[8,8]{1,0:T(8,128)S(1)}, s32[8,8]{1,0:T(8,128)}, u32[]{:S(2)}) copy-start(s32[8,8]{1,0:T(8,128)} %param.10) | copy-start | bytes 772
  64.9 10.8 %copy-start = (f32[8,64,512]{2,1,0:T(8,128)S(1)}, f32[8,64,512]{2,1,0:T(8,128)}, u32[]{:S(2)}) copy-start(f32[8,64,512]{2,1,0:T(8,128)} %param.8) | copy-start | bytes 3145732
  64.9 12.6 %copy-start.1 = (f32[8,64,128]{2,1,0:T(8,128)S(1)}, f32[8,64,128]{2,1,0:T(8,128)}, u32[]{:S(2)}) copy-start(f32[8,64,128]{2,1,0:T(8,128)} %param.14) | copy-start | bytes 786436
  65.0 12.9 %copy-start.3 = (s32[8,2]{0,1:T(2,128)S(1)}, s32[8,2]{0,1:T(2,128)}, u32[]{:S(2)}) copy-start(s32[8,2]{0,1:T(2,128)} %param.15) | copy-start | bytes 196
  65.0 104.8 %all-to-all-start.2 = ((f32[32,4,64,128]{3,2,1,0:T(8,128)}), f32[32,4,64,128]{3,2,1,0:T(8,128)}, u32[]{:S(2)}, u32[]{:S(2)}) async-start(f32[32,4,64,128]{3,2,1,0:T(8,128)} %bitcast.66), calls=%async_computation.2 | async-start | bytes 8388608 | tf_op jit(solution)/shard_map/all_to_all | solution.py:57
  75.4 3.7 copy-start.4
  75.4 345.9 %reduce-scatter.4.cloned.1.call-start = ((), (), s32[]{:S(2)}) async-start(), calls=%async_computation.5 | async-start | bytes 1081344
Sparse Core Ops, SparseCore 0:
  9.5 50.4 all-gather.2
  209.8 211.4 reduce-scatter.3
where the time goes:
time: 433 us; the launch traced here: 428 us
  waiting for transfers between devices  309 us (71%)
  starting transfers between devices  33.9 us (8%)
  matrix products  26.8 us (6%)
  local copies, waits for them, and re-layouts  25.8 us (6%)
  blocking collectives  18.6 us (4%)
  between operations  13.5 us (3%)
    unnamed x3, waiting for transfers between devices  212 us
    all_to_all x1, waiting for transfers between devices, local(): lax.all_to_all(fetched, 'col', split_axis=0, concat_axis=0, tiled=True)  89.6 us
    dot_general x4, matrix products, contract(): return jnp.einsum(form, left, right, precision=lax.Precision.HIGHEST)  26.8 us
    all_gather x1, blocking collectives, gather_panel(): lax.all_gather(prolong_cols, 'row', axis=0, tiled=True)  18.6 us
    all_to_all x1, starting transfers between devices, local(): lax.all_to_all(requests, 'col', split_axis=0, concat_axis=0, tiled=True)  13.7 us
    all_to_all x1, starting transfers between devices, local(): lax.all_to_all(fetched, 'col', split_axis=0, concat_axis=0, tiled=True)  10.4 us
    all_to_all x1, starting transfers between devices, local(): lax.all_to_all(fetched_columns, 'col', split_axis=0, concat_axis=0, tiled...  9.5 us
  transfers between devices with their start and end apart: 5, of which 3 were waited for; matrix products, arithmetic and copies ran while one was open for 3% of the time, Pallas kernels for 0%

commit v1 on v0

--- a/solution.py
+++ b/solution.py
@@ -69,9 +69,10 @@
         products.reshape(fine_rows, row_entries, block_size, prolong_entries, block_size),
         prolong_hot,
     )
-    partial_value = contract("iaQb,iaJc->QbJc", restrict_dense, product_dense)
-    partial_value = partial_value.reshape(NCR * block_size, coarse_all * block_size)
-    return lax.psum_scatter(partial_value, "col", scatter_dimension=1, tiled=True)
+    partial_value = contract("iaQb,iaJc->JcQb", restrict_dense, product_dense)
+    partial_value = partial_value.reshape(coarse_all, block_size, NCR * block_size)
+    shares = lax.all_to_all(partial_value, "col", split_axis=0, concat_axis=0, tiled=True)
+    return shares.sum(axis=0).T
 
 
 def solution(mesh):

time: 433 us -> 257 us (0.59)
  waiting for transfers between devices: 309 us -> 97.1 us
  blocking collectives: 18.6 us -> 51.8 us
  matrix products: 26.8 us -> 34.5 us
    unnamed x3 -> x1, waiting for transfers between devices: 212 us -> 0.71 us
    all_to_all x0 -> x1, blocking collectives: none -> 33.2 us  [local(): lax.all_to_all(partial_value, 'col', split_axis=0, concat_axis=0, tiled=T...]
    dot_general x4, matrix products: 26.8 us -> 34.5 us  [contract(): return jnp.einsum(form, left, right, precision=lax.Precision.HIGHEST)]
    unnamed x13 -> x11, local copies, waits for them, and re-layouts: 5.79 us -> 0.11 us
  transfers between devices with their start and end apart: 5 -> 4, of which waited for: 3 -> 2; matrix products, arithmetic and copies ran while one was open for 3% -> 5% of each run, Pallas kernels for 0% -> 0%
where the time goes in v1:
time: 257 us; the launch traced here: 254 us
  waiting for transfers between devices  97.1 us (38%)
  blocking collectives  51.8 us (20%)
  matrix products  34.5 us (13%)
  starting transfers between devices  33.8 us (13%)
  local copies, waits for them, and re-layouts  22.9 us (9%)
  between operations  13.5 us (5%)
    all_to_all x1, waiting for transfers between devices, local(): lax.all_to_all(fetched, 'col', split_axis=0, concat_axis=0, tiled=True)  88.9 us
    dot_general x4, matrix products, contract(): return jnp.einsum(form, left, right, precision=lax.Precision.HIGHEST)  34.5 us
    all_to_all x1, blocking collectives, local(): lax.all_to_all(partial_value, 'col', split_axis=0, concat_axis=0, tiled=T...  33.2 us
    all_gather x1, blocking collectives, gather_panel(): lax.all_gather(prolong_cols, 'row', axis=0, tiled=True)  18.6 us
    all_to_all x1, starting transfers between devices, local(): lax.all_to_all(requests, 'col', split_axis=0, concat_axis=0, tiled=True)  13.7 us
    all_to_all x1, starting transfers between devices, local(): lax.all_to_all(fetched, 'col', split_axis=0, concat_axis=0, tiled=True)  10.6 us
    all_to_all x1, starting transfers between devices, local(): lax.all_to_all(fetched_columns, 'col', split_axis=0, concat_axis=0, tiled...  9.5 us
    all_gather x1, waiting for transfers between devices, gather_panel(): lax.all_gather(prolong_blocks, 'row', axis=0, tiled=True)  7.48 us
  transfers between devices with their start and end apart: 4, of which 2 were waited for; matrix products, arithmetic and copies ran while one was open for 5% of the time, Pallas kernels for 0%

profile of v1, /device:TPU:1, one launch (start us, length us, event | category | flops | bytes accessed | tf_op | source)
XLA Modules:
  0.0 254.5 jit_solution(7941027741870948165)
XLA Ops:
  6.5 0.7 all-gather.3.cloned.1.call-update
  7.3 1.4 copy.23
  8.6 13.7 %all-to-all-start = ((s32[32,1,4]{2,1,0:T(1,128)}), s32[32,1,4]{2,1,0:T(1,128)S(1)}, u32[]{:S(2)}, u32[]{:S(2)}) async-start(s32[32,1,4]{2,1,0:T(1,128)} %copy.23), calls=%async_computation | async-start | bytes 32768 | tf_op jit(solution)/shard_map/all_to_all | solution.py:53
  22.3 18.6 %all-gather = s32[16,8,2]{1,2,0:T(2,128)S(1)} all-gather(s32[1,8,2]{1,2,0:T(2,128)} %bitcast.68), channel_id=1, replica_groups=mesh['row'=16,'col'=32] {'row'}, dimensions={0}, use_global_device_ids=true | all-gather | bytes 1088 | tf_op jit(solution)/shard_map/all_gather | solution.py:16
  41.4 0.6 gather_fusion
  42.1 0.9 copy.26
  43.0 9.5 %all-to-all-start.1 = ((s32[32,4,2]{1,2,0:T(2,128)}), s32[32,4,2]{1,2,0:T(2,128)S(1)}, u32[]{:S(2)}, u32[]{:S(2)}) async-start(s32[32,4,2]{1,2,0:T(2,128)} %copy.26), calls=%async_computation.1 | async-start | bytes 65536 | tf_op jit(solution)/shard_map/all_to_all | solution.py:58
  52.5 7.5 %all-gather.3.cloned.1.call-done = f32[128,64,128]{2,1,0:T(8,128)} async-done(((f32[8,64,128]{2,1,0:T(8,128)}), f32[128,64,128]{2,1,0:T(8,128)}) %all-gather.3.cloned.1.call-update) | async-done | bytes 4194320 | tf_op jit(solution)/shard_map/all_gather | solution.py:15
  60.0 5.0 %gather_fusion.2 = f32[128,64,128]{2,1,0:T(8,128)} fusion(f32[128,64,128]{2,1,0:T(8,128)} %all-gather.3.cloned.1.call-done, s32[1024]{0:T(1024)S(1)} %pad_clamp_fusion.1), kind=kCustom, calls=%fused_computation.2 | custom fusion | bytes 8389120 | tf_op jit(solution)/shard_map/gather | solution.py:55
  65.0 10.6 %all-to-all-start.2 = ((f32[32,4,64,128]{3,2,1,0:T(8,128)}), f32[32,4,64,128]{3,2,1,0:T(8,128)}, u32[]{:S(2)}, u32[]{:S(2)}) async-start(f32[32,4,64,128]{3,2,1,0:T(8,128)} %bitcast.61), calls=%async_computation.2 | async-start | bytes 8388608 | tf_op jit(solution)/shard_map/all_to_all | solution.py:57
  75.7 1.8 reshape.166
  77.5 0.3 reshape.168
  78.0 1.1 convolution_bitcast_fusion
  79.4 0.6 gather_fusion.1
  80.1 88.9 %all-to-all-done.2 = f32[32,4,64,128]{3,2,1,0:T(8,128)} async-done(((f32[32,4,64,128]{3,2,1,0:T(8,128)}), f32[32,4,64,128]{3,2,1,0:T(8,128)}, u32[]{:S(2)}, u32[]{:S(2)}) %all-to-all-start.2) | async-done | bytes 4194336 | tf_op jit(solution)/shard_map/all_to_all | solution.py:57
  169.0 2.9 %gather_fusion.3 = f32[64,64,128]{2,1,0:T(8,128)S(1)} fusion(f32[128,64,128]{2,1,0:T(8,128)} %bitcast.10, s32[1024]{0:T(1024)S(1)} %pad_clamp_fusion), kind=kCustom, calls=%fused_computation.3 | custom fusion | bytes 4194560 | tf_op jit(solution)/shard_map/gather | solution.py:61
  171.9 5.2 %fusion.12 = f32[8,8,64,128]{3,2,1,0:T(8,128)} fusion(f32[8,8,64,128]{3,2,1,0:T(8,128)S(1)} %bitcast.62, f32[8,64,8,64]{3,2,1,0:T(8,128)} %reshape.166), kind=kOutput, calls=%fused_computation.12 | convolution fusion | flops 402653184 | bytes 5242880 | tf_op jit(solution)/shard_map/iakb,ikbn->ikan/dot_general | solution.py:10
  177.1 5.6 %reshape.167 = f32[8,8,64,2,64]{4,3,2,1,0:T(2,128)} reshape(f32[8,8,64,128]{3,2,1,0:T(8,128)} %fusion.12) | data formatting | bytes 4194304 | tf_op jit(solution)/shard_map/reshape | solution.py:69
  182.7 11.2 %fusion.4 = f32[8,64,32,64,1]{3,2,1,0,4:T(8,128)S(1)} fusion(f32[8,8,64,2,64]{4,3,2,1,0:T(2,128)} %reshape.167, f32[8,8]{1,0:T(8,128)S(1)} %fusion.26, s32[8,8,2]{1,2,0:T(2,128)S(1)} %copy.29), kind=kOutput, calls=%fused_computation.8 | convolution fusion | flops 201334784 | bytes 6292224 | tf_op jit(solution)/shard_map/ikamc,ikmJ->iaJc/dot_general | solution.py:10
  193.9 17.1 %fusion.9 = f32[32,64,2,64]{3,1,2,0:T(8,128)S(1)} fusion(f32[8,64,32,64,1]{3,2,1,0,4:T(8,128)S(1)} %fusion.4, f32[8,64,2,64]{3,2,1,0:T(2,128)S(1)} %convolution_bitcast_fusion), kind=kOutput, calls=%fused_computation.11 | convolution fusion | flops 1610612736 | bytes 5505024 | tf_op jit(solution)/shard_map/iaQb,iaJc->JcQb/dot_general | solution.py:10
  211.0 1.7 copy.35
  212.7 1.1 reshape.169
  213.8 33.2 %all_to_all.27 = f32[32,64,128]{2,1,0:T(8,128)S(1)} all-to-all(f32[32,64,128]{2,1,0:T(8,128)S(1)} %reshape.169), channel_id=1, replica_groups=mesh['row'=16,'col'=32] {'col'}, dimensions={0} | all-to-all | bytes 2097152 | tf_op jit(solution)/shard_map/all_to_all | solution.py:74
  246.9 0.7 reduce_sum.9
  (26 shorter events, 1.2 us)
Async XLA Ops:
  6.5 53.5 %all-gather.3.cloned.1.call-start = ((), (), s32[]{:S(2)}) async-start(), calls=%async_computation.4 | async-start | bytes 4456448 | tf_op jit(solution)/shard_map/all_gather | solution.py:15
  8.6 32.5 %all-to-all-start = ((s32[32,1,4]{2,1,0:T(1,128)}), s32[32,1,4]{2,1,0:T(1,128)S(1)}, u32[]{:S(2)}, u32[]{:S(2)}) async-start(s32[32,1,4]{2,1,0:T(1,128)} %copy.23), calls=%async_computation | async-start | bytes 32768 | tf_op jit(solution)/shard_map/all_to_all | solution.py:53
  43.0 21.9 %all-to-all-start.1 = ((s32[32,4,2]{1,2,0:T(2,128)}), s32[32,4,2]{1,2,0:T(2,128)S(1)}, u32[]{:S(2)}, u32[]{:S(2)}) async-start(s32[32,4,2]{1,2,0:T(2,128)} %copy.26), calls=%async_computation.1 | async-start | bytes 65536 | tf_op jit(solution)/shard_map/all_to_all | solution.py:58
  64.9 10.6 %copy-start.2 = (s32[8,8]{1,0:T(8,128)S(1)}, s32[8,8]{1,0:T(8,128)}, u32[]{:S(2)}) copy-start(s32[8,8]{1,0:T(8,128)} %param.10) | copy-start | bytes 772
  64.9 10.7 %copy-start = (f32[8,64,512]{2,1,0:T(8,128)S(1)}, f32[8,64,512]{2,1,0:T(8,128)}, u32[]{:S(2)}) copy-start(f32[8,64,512]{2,1,0:T(8,128)} %param.8) | copy-start | bytes 3145732
  65.0 12.5 %copy-start.1 = (f32[8,64,128]{2,1,0:T(8,128)S(1)}, f32[8,64,128]{2,1,0:T(8,128)}, u32[]{:S(2)}) copy-start(f32[8,64,128]{2,1,0:T(8,128)} %param.14) | copy-start | bytes 786436
  65.0 12.9 %copy-start.3 = (s32[8,2]{0,1:T(2,128)S(1)}, s32[8,2]{0,1:T(2,128)}, u32[]{:S(2)}) copy-start(s32[8,2]{0,1:T(2,128)} %param.15) | copy-start | bytes 196
  65.0 13.0 %copy-start.4 = (s32[8]{0:T(128)S(1)}, s32[8]{0:T(128)}, u32[]{:S(2)}) copy-start(s32[8]{0:T(128)} %param.9) | copy-start | bytes 100
  65.0 104.0 %all-to-all-start.2 = ((f32[32,4,64,128]{3,2,1,0:T(8,128)}), f32[32,4,64,128]{3,2,1,0:T(8,128)}, u32[]{:S(2)}, u32[]{:S(2)}) async-start(f32[32,4,64,128]{3,2,1,0:T(8,128)} %bitcast.61), calls=%async_computation.2 | async-start | bytes 8388608 | tf_op jit(solution)/shard_map/all_to_all | solution.py:57
Sparse Core Ops, SparseCore 0:
  9.5 50.4 all-gather.2

commit v2 on v0

v2 whole, which is shorter than its diff:
```python
import functools

import jax
import jax.numpy as jnp
from jax import lax
from jax.experimental import pallas as pl
from jax.experimental.pallas import tpu as pltpu
from jax.sharding import PartitionSpec as P

MESH = pl.DeviceIdType.MESH
F32 = jnp.float32
BF16 = jnp.bfloat16

NX, NZ = 4, 8
CORES = 2
NCR = 2
FBD = 8
SLOT = 4
BS = 64
HALF = BS // 2


class Geometry:
    def __init__(self, rows, cols, x=NX, z=NZ, slot=SLOT):
        self.rows, self.cols, self.x, self.z, self.slot = rows, cols, x, z, slot
        self.y = rows // CORES
        self.pair = z * slot // rows
        self.out_y = slot * HALF + 8
        self.out_z = self.pair * (BS - HALF)


def half_ring(n):
    return n // 2, n - 1 - n // 2


def fetch_kernel(
    g, idxy_ref, idxz_ref, p_ref, tag_ref, gy_ref, gz_ref,
    pan_y, pan_z, pan_t, st_y, st_z, iy, iz, sy, sz,
    yu_s, yu_r, yd_s, yd_r, zu_s, zu_r, zd_s, zd_r, sib_s, sib_r,
    ix_s, ix_r, ex_s, ex_r, loc,
):
    me_r, me_c = lax.axis_index("row"), lax.axis_index("col")
    y, core = me_r // CORES, me_r % CORES
    x, z = me_c // g.z, me_c % g.z
    low = BS - HALF

    def peer_y(t, sign):
        dx, dz = t // g.z, t % g.z
        px = (x + sign * dx + g.x) % g.x
        pz = (z + sign * dz + g.z) % g.z
        return px * g.z + pz

    def peer_z(t, sign):
        dr, dx = t // g.x, t % g.x
        pr = (me_r + sign * dr + g.rows) % g.rows
        px = (x + sign * dx + g.x) % g.x
        return pr, px

    n_y, n_z = g.cols, g.rows * g.x
    barrier = pltpu.get_barrier_semaphore()

    @pl.loop(1, n_y)
    def _(t):
        pl.semaphore_signal(barrier, inc=1, device_id=(me_r, peer_y(t, 1)), device_id_type=MESH)

    @pl.loop(1, n_z)
    def _(t):
        pr, px = peer_z(t, 1)
        pl.semaphore_signal(barrier, inc=1, device_id=(pr, px * g.z + z), device_id_type=MESH)

    for j in range(FBD):
        pan_y[me_r * FBD + j] = p_ref[j, 0:HALF, :]
        pan_z[z * FBD + j] = p_ref[j, HALF:BS, :]
        pan_t[j] = tag_ref[j]
    iy[0] = idxy_ref[me_c]
    iz[0] = idxz_ref[me_r * g.x + x]

    pl.semaphore_wait(barrier, n_y - 1 + n_z - 1)

    def row_of(yy):
        return ((yy + g.y) % g.y) * CORES + core

    def ring_y(t, sign, send, recv):
        src = pan_y.at[pl.ds(row_of(y - sign * (t - 1)) * FBD, FBD)]
        dst_row = row_of(y + sign)
        return pltpu.make_async_remote_copy(
            src_ref=src, dst_ref=src, send_sem=send.at[t - 1], recv_sem=recv.at[t - 1],
            device_id=(dst_row, me_c), device_id_type=MESH,
        )

    def ring_z(t, sign, send, recv):
        at = (z - sign * (t - 1) + g.z) % g.z
        src = pan_z.at[pl.ds(at * FBD, FBD)]
        return pltpu.make_async_remote_copy(
            src_ref=src, dst_ref=src, send_sem=send.at[t - 1], recv_sem=recv.at[t - 1],
            device_id=(me_r, x * g.z + (z + sign + g.z) % g.z), device_id_type=MESH,
        )

    def sibling(yy, slot):
        src = pan_y.at[pl.ds(row_of(yy) * FBD, FBD)]
        return pltpu.make_async_remote_copy(
            src_ref=src, dst_ref=src, send_sem=sib_s.at[slot], recv_sem=sib_r.at[slot],
            device_id=(y * CORES + (1 - core), me_c), device_id_type=MESH,
        )

    up_y, down_y = half_ring(g.y)
    up_z, down_z = half_ring(g.z)
    rings = [
        (ring_y, 1, up_y, yu_s, yu_r), (ring_z, 1, up_z, zu_s, zu_r),
        (ring_y, -1, down_y, yd_s, yd_r), (ring_z, -1, down_z, zd_s, zd_r),
    ]
    for make, sign, steps, send, recv in rings:
        if steps:
            make(1, sign, send, recv).start()
    sibs = [sibling(y, 0)]
    sibs[0].start()

    @pl.loop(1, g.rows)
    def _(d):
        pltpu.make_async_remote_copy(
            src_ref=tag_ref, dst_ref=pan_t.at[pl.ds(d * FBD, FBD)], send_sem=ix_s.at[2], recv_sem=ix_r.at[2],
            device_id=((me_r - d + g.rows) % g.rows, me_c), device_id_type=MESH,
        ).start()

    @pl.loop(1, n_y)
    def _(t):
        dev = peer_y(t, -1)
        pltpu.make_async_remote_copy(
            src_ref=idxy_ref.at[dev], dst_ref=iy.at[t], send_sem=ix_s.at[0], recv_sem=ix_r.at[0],
            device_id=(me_r, dev), device_id_type=MESH,
        ).start()

    @pl.loop(1, n_z)
    def _(t):
        pr, px = peer_z(t, -1)
        pltpu.make_async_remote_copy(
            src_ref=idxz_ref.at[pr * g.x + px], dst_ref=iz.at[t], send_sem=ix_s.at[1], recv_sem=ix_r.at[1],
            device_id=(pr, px * g.z + z), device_id_type=MESH,
        ).start()

    for t in range(1, max(up_y, up_z) + 1):
        for make, sign, steps, send, recv in rings:
            if t <= steps:
                make(t, sign, send, recv).wait_recv()
                if t < steps:
                    make(t + 1, sign, send, recv).start()
                if make is ring_y:
                    copy = sibling(y - sign * t, len(sibs))
                    copy.start()
                    sibs.append(copy)

    def all_of(buf, count, send, recv, unit=1):
        view = buf.at[pl.ds(unit, (count - 1) * unit)]
        return pltpu.make_async_remote_copy(
            src_ref=view, dst_ref=view, send_sem=send, recv_sem=recv,
            device_id=(me_r, me_c), device_id_type=MESH,
        )

    all_of(iy, n_y, ix_s.at[0], ix_r.at[0]).wait_recv()
    all_of(iz, n_z, ix_s.at[1], ix_r.at[1]).wait_recv()
    all_of(pan_t, g.rows, ix_s.at[2], ix_r.at[2], FBD).wait_recv()
    to_sy = pltpu.make_async_copy(iy, sy, loc.at[0])
    to_sz = pltpu.make_async_copy(iz, sz, loc.at[1])
    to_sy.start()
    to_sz.start()
    to_sy.wait()
    to_sz.wait()
    for copy in sibs:
        copy.wait_recv()

    def stage_y(t):
        for s in range(g.slot):
            st_y[t, s * HALF:(s + 1) * HALF, :] = pan_y[sy[t, 0, s]]
            tag = pan_t[sy[t, 0, g.slot + s]]
            for rep in range(8 // g.slot):
                row = g.slot * HALF + rep * g.slot + s
                st_y[t, row:row + 1, :] = tag

    def stage_z(t):
        for s in range(g.pair):
            st_z[t, s * low:(s + 1) * low, :] = pan_z[sz[t, 0, s]]

    def send_y(q):
        t = (q * 13) % n_y
        stage_y(t)
        pltpu.make_async_remote_copy(
            src_ref=st_y.at[t], dst_ref=gy_ref.at[t], send_sem=ex_s.at[0], recv_sem=ex_r.at[0],
            device_id=(me_r, peer_y(t, 1)), device_id_type=MESH,
        ).start()

    def send_z(q):
        t = (q * 29) % n_z
        stage_z(t)
        pr, px = peer_z(t, 1)
        pltpu.make_async_remote_copy(
            src_ref=st_z.at[t], dst_ref=gz_ref.at[t], send_sem=ex_s.at[1], recv_sem=ex_r.at[1],
            device_id=(pr, px * g.z + z), device_id_type=MESH,
        ).start()

    ratio = n_z // n_y

    @pl.loop(1, n_y)
    def _(q):
        send_y(q)
        for j in range(ratio):
            send_z(ratio * q - j)

    for j in range(1, ratio):
        send_z(n_z - j)

    stage_y(0)
    stage_z(0)
    own_a = pltpu.make_async_copy(st_y.at[0], gy_ref.at[0], loc.at[2])
    own_b = pltpu.make_async_copy(st_z.at[0], gz_ref.at[0], loc.at[3])
    own_a.start()
    own_b.start()

    for make, sign, steps, send, recv in rings:
        for t in range(1, steps + 1):
            make(t, sign, send, recv).wait_send()
    for copy in sibs:
        copy.wait_send()
    all_of(iy, n_y, ix_s.at[0], ix_r.at[0]).wait_send()
    all_of(iz, n_z, ix_s.at[1], ix_r.at[1]).wait_send()
    all_of(pan_t, g.rows, ix_s.at[2], ix_r.at[2], FBD).wait_send()
    own_a.wait()
    own_b.wait()
    all_of(st_y, n_y, ex_s.at[0], ex_r.at[0]).wait_send()
    all_of(st_z, n_z, ex_s.at[1], ex_r.at[1]).wait_send()
    all_of(gy_ref, n_y, ex_s.at[0], ex_r.at[0]).wait_recv()
    all_of(gz_ref, n_z, ex_s.at[1], ex_r.at[1]).wait_recv()


def fetch(g, idxy, idxz, prolong_blocks, tags):
    up_y, down_y = half_ring(g.y)
    up_z, down_z = half_ring(g.z)
    dma = pltpu.SemaphoreType.DMA
    n_y, n_z = g.cols, g.rows * g.x
    vmem = pl.BlockSpec(memory_space=pltpu.VMEM)
    return pl.pallas_call(
        functools.partial(fetch_kernel, g),
        out_shape=(
            jax.ShapeDtypeStruct((n_y, g.out_y, 128), F32),
            jax.ShapeDtypeStruct((n_z, g.out_z, 128), F32),
        ),
        in_specs=[vmem] * 4,
        out_specs=(pl.BlockSpec(memory_space=pl.ANY),) * 2,
        scratch_shapes=[
            pltpu.VMEM((g.rows * FBD, HALF, 128), F32),
            pltpu.VMEM((g.z * FBD, BS - HALF, 128), F32),
            pltpu.VMEM((g.rows * FBD, 1, 128), F32),
            pltpu.VMEM((n_y, g.out_y, 128), F32),
            pltpu.VMEM((n_z, g.out_z, 128), F32),
            pltpu.VMEM((n_y, 1, 128), jnp.int32),
            pltpu.VMEM((n_z, 1, 128), jnp.int32),
            pltpu.SMEM((n_y, 1, 128), jnp.int32),
            pltpu.SMEM((n_z, 1, 128), jnp.int32),
            dma((up_y,)), dma((up_y,)), dma((max(down_y, 1),)), dma((max(down_y, 1),)),
            dma((up_z,)), dma((up_z,)), dma((max(down_z, 1),)), dma((max(down_z, 1),)),
            dma((g.y,)), dma((g.y,)),
            dma((3,)), dma((3,)), dma((2,)), dma((2,)), dma((4,)),
        ],
        compiler_params=pltpu.CompilerParams(
            collective_id=0, has_side_effects=True, vmem_limit_bytes=32 << 20
        ),
        name="fetch",
    )(idxy, idxz, prolong_blocks, tags)


def split(value):
    high = value.astype(BF16)
    return high, (value - high.astype(F32)).astype(BF16)


def dot_t(left, right):
    return lax.dot_general(left, right, (((0,), (0,)), ((), ())), preferred_element_type=F32)


def product_kernel(
    g, fetch_ref, slot_ref, count_ref, rows_ref, a_ref, r_ref, gy_hbm, gz_hbm, acc_ref,
    gy, gz, tags, w, sem,
):
    me_r, me_c = lax.axis_index("row"), lax.axis_index("col")
    x, z = me_c // g.z, me_c % g.z
    n_i, _, width = a_ref.shape
    n_k = width // BS
    low = BS - HALF
    copies = [
        pltpu.make_async_copy(gy_hbm, gy, sem.at[0]),
        pltpu.make_async_copy(gz_hbm, gz, sem.at[1]),
        pltpu.make_async_copy(gy_hbm.at[:, pl.ds(g.slot * HALF, 8), :], tags, sem.at[2]),
    ]
    for copy in copies:
        copy.start()
    acc_ref[...] = jnp.zeros_like(acc_ref)
    lane = lax.broadcasted_iota(jnp.int32, (BS, 2 * BS), 1) // BS

    @pl.loop(0, n_i)
    def _(i):
        stored = r_ref[i]
        swapped = pltpu.roll(stored, BS, 1)
        first, second = rows_ref[i, 0], rows_ref[i, 1]
        own = jnp.where(lane == 0, first, second)
        other = jnp.where(lane == 0, second, first)
        dense = jnp.where(own == lane, stored, 0.0) + jnp.where(other == lane, swapped, 0.0)
        r_hi, r_lo = split(dense)
        a_hi, a_lo = split(a_ref[i])
        ra = dot_t(
            jnp.concatenate([a_hi, a_lo, a_hi], axis=0),
            jnp.concatenate([r_hi, r_hi, r_lo], axis=0),
        )
        for k in range(n_k):
            part = jnp.where(k < count_ref[i], ra[k * BS:(k + 1) * BS, :], 0.0)
            hi, lo = split(part)
            at = i * n_k + k
            w[at, 0:BS, :] = hi
            w[at, BS:2 * BS, :] = hi
            w[at, 2 * BS:3 * BS, :] = lo

    for copy in copies:
        copy.wait()

    @pl.loop(0, n_i)
    def _(i):
        for k in range(n_k):
            slot = slot_ref[i, k]
            peer, s = slot // g.slot, slot % g.slot
            px, pz = peer // g.z, peer % g.z
            owner_row = fetch_ref[peer, s] // (FBD * g.cols)
            dx = (x - px + g.x) % g.x
            t = dx * g.z + (z - pz + g.z) % g.z
            tz = ((me_r - owner_row + g.rows) % g.rows) * g.x + dx
            j = pz // (g.z // g.pair)
            top = gy[t, pl.ds(pl.multiple_of(s * HALF, 8), HALF), :]
            bottom = gz[tz, pl.ds(pl.multiple_of(j * low, 8), low), :]
            p_hi, p_lo = split(jnp.concatenate([top, bottom], axis=0))
            out = dot_t(jnp.concatenate([p_hi, p_lo, p_hi], axis=0), w[i * n_k + k])
            first = tags[t, s, 0].astype(jnp.int32)
            second = tags[t, s, BS].astype(jnp.int32)
            acc_ref[first] += out[0:BS, :]
            acc_ref[second] += out[BS:2 * BS, :]


def product(g, requests, slots, counts, rows, blocks, restrict, gy, gz):
    n_i, _, width = blocks.shape
    n_k = width // BS
    smem = pl.BlockSpec(memory_space=pltpu.SMEM)
    vmem = pl.BlockSpec(memory_space=pltpu.VMEM)
    hbm = pl.BlockSpec(memory_space=pl.ANY)
    return pl.pallas_call(
        functools.partial(product_kernel, g),
        out_shape=jax.ShapeDtypeStruct((NCR * g.rows, BS, NCR * BS), F32),
        in_specs=[smem] * 4 + [vmem] * 2 + [hbm] * 2,
        out_specs=vmem,
        scratch_shapes=[
            pltpu.VMEM(gy.shape, F32),
            pltpu.VMEM(gz.shape, F32),
            pltpu.SMEM((g.cols, 8, 128), F32),
            pltpu.VMEM((n_i * n_k, 3 * BS, NCR * BS), BF16),
            pltpu.SemaphoreType.DMA((3,)),
        ],
        compiler_params=pltpu.CompilerParams(vmem_limit_bytes=32 << 20),
        name="product",
    )(requests, slots, counts, rows, blocks, restrict, gy, gz)


def reduce_kernel(g, acc_ref, o_ref, r1, s1, r2, s1_send, s1_recv, s2_send, s2_recv):
    me_r, me_c = lax.axis_index("row"), lax.axis_index("col")
    x, z = me_c // g.z, me_c % g.z
    per = acc_ref.shape[0] // g.cols
    barrier = pltpu.get_barrier_semaphore()

    def col_x(dx):
        return ((x + dx) % g.x) * g.z + z

    def col_z(dz):
        return x * g.z + (z + dz) % g.z

    for dx in range(1, g.x):
        pl.semaphore_signal(barrier, inc=1, device_id=(me_r, col_x(dx)), device_id_type=MESH)
    for dz in range(1, g.z):
        pl.semaphore_signal(barrier, inc=1, device_id=(me_r, col_z(dz)), device_id_type=MESH)
    pl.semaphore_wait(barrier, g.x + g.z - 2)

    order = sorted(range(g.z), key=lambda dz: -min(dz, g.z - dz))
    first = []
    for dz in order:
        for dx in range(1, g.x):
            tile = ((x + dx) % g.x) * g.z + (z + dz) % g.z
            copy = pltpu.make_async_remote_copy(
                src_ref=acc_ref.at[pl.ds(tile * per, per)], dst_ref=r1.at[dz, dx - 1],
                send_sem=s1_send.at[dz, dx - 1], recv_sem=s1_recv.at[dz, dx - 1],
                device_id=(me_r, col_x(dx)), device_id_type=MESH,
            )
            copy.start()
            first.append((dz, copy))
    second = []
    for dz in order:
        for at, copy in first:
            if at == dz:
                copy.wait_recv()
        tile = x * g.z + (z + dz) % g.z
        total = acc_ref[pl.ds(tile * per, per)]
        for dx in range(1, g.x):
            total = total + r1[dz, dx - 1]
        s1[dz] = total
        if dz:
            copy = pltpu.make_async_remote_copy(
                src_ref=s1.at[dz], dst_ref=r2.at[dz - 1],
                send_sem=s2_send.at[dz - 1], recv_sem=s2_recv.at[dz - 1],
                device_id=(me_r, col_z(dz)), device_id_type=MESH,
            )
            copy.start()
            second.append((dz, copy))
    total = s1[0]
    for dz, copy in second:
        copy.wait_recv()
        total = total + r2[dz - 1]
    o_ref[...] = total
    for _, copy in first + second:
        copy.wait_send()


def reduce(g, acc):
    tile = acc.shape[1:]
    per = acc.shape[0] // g.cols
    vmem = pl.BlockSpec(memory_space=pltpu.VMEM)
    dma = pltpu.SemaphoreType.DMA
    return pl.pallas_call(
        functools.partial(reduce_kernel, g),
        out_shape=jax.ShapeDtypeStruct((per,) + tile, F32),
        in_specs=[vmem],
        out_specs=vmem,
        scratch_shapes=[
            pltpu.VMEM((g.z, max(g.x - 1, 1), per) + tile, F32),
            pltpu.VMEM((g.z, per) + tile, F32),
            pltpu.VMEM((g.z - 1, per) + tile, F32),
            dma((g.z, max(g.x - 1, 1))), dma((g.z, max(g.x - 1, 1))),
            dma((g.z - 1,)), dma((g.z - 1,)),
        ],
        compiler_params=pltpu.CompilerParams(collective_id=1, has_side_effects=True),
        name="reduce",
    )(acc)


def request_tables(g, requests):
    owner_row = requests // (FBD * g.cols)
    inside = requests % FBD
    turn = (owner_row - lax.axis_index("row") + g.rows) % g.rows
    idxy = jnp.concatenate([owner_row * FBD + inside, turn * FBD + inside], axis=1)
    idxy = jnp.pad(idxy, ((0, 0), (0, 128 - 2 * g.slot)))[:, None, :]
    zz = (jnp.arange(g.cols, dtype=jnp.int32) % g.z)[:, None]
    at = zz * FBD + inside
    per = g.z // g.pair * g.slot
    owner_row = owner_row.reshape(1, g.x, g.pair, per)
    at = at.reshape(1, g.x, g.pair, per)
    rows = jnp.arange(g.rows, dtype=jnp.int32)[:, None, None, None]
    idxz = jnp.where(owner_row == rows, at, 0).sum(axis=-1)
    idxz = jnp.pad(idxz.reshape(g.rows * g.x, g.pair), ((0, 0), (0, 128 - g.pair)))[:, None, :]
    return idxy, idxz


def local(
    g,
    operator_blocks,
    operator_count,
    operator_slot,
    fetch_lists,
    prolong_blocks,
    prolong_cols,
    restrict_blocks,
    restrict_rows,
):
    requests = fetch_lists.reshape(g.cols, g.slot)
    idxy, idxz = request_tables(g, requests)
    tags = jnp.repeat(prolong_cols.astype(F32), BS, axis=1)[:, None, :]
    gy, gz = fetch(g, idxy, idxz, prolong_blocks, tags)
    acc = product(
        g, requests, operator_slot, operator_count, restrict_rows, operator_blocks, restrict_blocks, gy, gz
    )
    share = reduce(g, acc)
    return share.reshape(-1, NCR * BS).T


def solution(mesh):
    g = Geometry(mesh.shape["row"], mesh.shape["col"])
    return jax.shard_map(
        functools.partial(local, g),
        mesh=mesh,
        in_specs=(
            P(("row", "col"), None, None),
            P(("row", "col")),
            P(("row", "col"), None),
            P("row", "col", None, None),
            P(("row", "col"), None, None),
            P(("row", "col"), None),
            P(("row", "col"), None, None),
            P(("row", "col"), None),
        ),
        out_specs=P("row", "col"),
        check_vma=False,
    )
```

time: 433 us -> 131 us (0.30)
  waiting for transfers between devices: 309 us -> 0 us
  Pallas kernels: 0 us -> 118 us
  starting transfers between devices: 33.9 us -> 0 us
  matrix products: 26.8 us -> 0 us
  blocking collectives: 18.6 us -> 0 us
  local copies, waits for them, and re-layouts: 25.8 us -> 9.77 us
  between operations: 13.5 us -> 0.07 us
    unnamed x3 -> x0, waiting for transfers between devices: 212 us -> none
    pallas_call x0 -> x3, Pallas kernels: none -> 118 us  [the longest x1 86.3 us: fetch(): pl.pallas_call(functools.partial(fetch_kernel, g), out_shape=(jax.ShapeDt...]
    all_to_all x3 -> x0, waiting for transfers between devices: 89.6 us -> none  [the longest x1 89.6 us: local(): lax.all_to_all(fetched, 'col', split_axis=0, concat_axis=0, tiled=True)]
    all_to_all x3 -> x0, starting transfers between devices: 33.6 us -> none  [the longest x1 13.7 us: local(): lax.all_to_all(requests, 'col', split_axis=0, concat_axis=0, tiled=True)]
    dot_general x4 -> x0, matrix products: 26.8 us -> none  [contract(): return jnp.einsum(form, left, right, precision=lax.Precision.HIGHEST)]
    all_gather x1 -> x0, blocking collectives: 18.6 us -> none  [gather_panel(): lax.all_gather(prolong_cols, 'row', axis=0, tiled=True)]
    gather x6 -> x0, local copies, waits for them, and re-layouts: 10.1 us -> none  [the longest x1 4.95 us: local(): fetched = panel_blocks[position]]
    all_gather x1 -> x0, waiting for transfers between devices: 7.48 us -> none  [gather_panel(): lax.all_gather(prolong_blocks, 'row', axis=0, tiled=True)]
  transfers between devices with their start and end apart: 5 -> 0, of which waited for: 3 -> 0; matrix products, arithmetic and copies ran while one was open for 3% -> 0% of each run, Pallas kernels for 0% -> 0%
where the time goes in v2:
time: 131 us; the launch traced here: 130 us
  Pallas kernels  118 us (90%)
  local copies, waits for them, and re-layouts  9.77 us (7%)
  other arithmetic  1.64 us (1%)
    pallas_call x1, Pallas kernels, fetch(): pl.pallas_call(functools.partial(fetch_kernel, g), out_shape=(jax.ShapeDt...  86.3 us
    pallas_call x1, Pallas kernels, reduce(): pl.pallas_call(functools.partial(reduce_kernel, g), out_shape=jax.ShapeDt...  23.9 us
    unnamed x15, local copies, waits for them, and re-layouts  8.31 us
    pallas_call x1, Pallas kernels, product(): pl.pallas_call(functools.partial(product_kernel, g), out_shape=jax.ShapeD...  8.21 us

profile of v2, /device:TPU:1, one launch (start us, length us, event | category | flops | bytes accessed | tf_op | source)
XLA Modules:
  0.0 129.9 jit_solution(10768330968633063053)
XLA Ops:
  0.0 0.7 convert_element_type.3
  0.7 0.1 copy.37
  0.8 0.7 multiply_add_fusion
  1.5 0.1 broadcast_in_dim.27
  1.6 0.1 broadcast_in_dim_reshape.3.tag_ref
  1.6 0.8 copy.39.rows_ref
  2.4 0.1 add.70
  2.5 0.1 add.71
  2.6 0.1 copy.33
  2.7 0.8 copy.38.fetch_ref
  3.4 0.8 copy.34
  4.2 0.1 reshape.84
  4.3 0.2 select_reduce_fusion
  4.5 0.1 copy.40
  4.7 0.9 copy-done.2
  5.6 86.3 %fetch.1 = (f32[32,136,128]{2,1,0:T(8,128)S(1)}, f32[64,64,128]{2,1,0:T(8,128)S(1)}) custom-call(s32[32,1,128]{2,1,0:T(1,128)S(1)} %bitcast.20, s32[64,1,128]{2,1,0:T(1,128)S(1)} %bitcast.19, f32[8,64,128]{2,1,0:T(8,128)S(1)} %copy-done.2, f32[8,1,128]{2,1,0:T(1,128)S(1)} %broadcast_in_dim_reshape.3.tag_ref), custom_call_target="tpu_custom_call" | custom-call | tf_op jit(solution)/shard_map/fetch/pallas_call | solution.py:240
  92.0 1.2 copy-done.1
  93.2 0.9 copy-done.3
  94.1 0.7 copy-done.4
  94.8 0.7 copy-done.5
  95.5 8.2 %product.1.acc_ref = f32[32,64,128]{2,1,0:T(8,128)S(1)} custom-call(s32[32,4]{1,0:T(8,128)S(1)} %copy.38.fetch_ref, s32[8,8]{1,0:T(8,128)S(1)} %copy-done.4, s32[8]{0:T(128)S(1)} %copy-done.5, s32[8,2]{1,0:T(8,128)S(1)} %copy.39.rows_ref, f32[8,64,512]{2,1,0:T(8,128)S(1)} %copy-done.1, f32[8,64,128]{2,1,0:T(8,128)S(1)} %copy-done.3, ...), custom_call_target="tpu_custom_call" | custom-call | tf_op jit(solution)/shard_map/product/pallas_call | solution.py:350
  103.7 1.0 copy-done
  104.7 23.9 %reduce.1 = f32[1,64,128]{2,1,0:T(8,128)} custom-call(f32[32,64,128]{2,1,0:T(8,128)} %copy-done), custom_call_target="tpu_custom_call" | custom-call | tf_op jit(solution)/shard_map/reduce/pallas_call | solution.py:429
  128.5 1.4 %copy.43 = f32[128,64]{0,1:T(8,128)} copy(f32[128,64]{0,1:T(8,128)} %bitcast.21) | data formatting | bytes 65536
  (11 shorter events, 0.1 us)
Async XLA Ops:
  4.6 1.0 copy-start.2
  91.9 1.2 copy-start.1
  93.2 0.9 copy-start.3
  94.1 0.7 copy-start.4
  94.8 0.7 copy-start.5
  103.7 1.0 copy-start

commit v3 on v0

v3 whole, which is shorter than its diff:
```python
import functools

import jax
import jax.numpy as jnp
from jax import lax
from jax.experimental import pallas as pl
from jax.experimental.pallas import tpu as pltpu
from jax.sharding import PartitionSpec as P

MESH = pl.DeviceIdType.MESH
F32 = jnp.float32
BF16 = jnp.bfloat16

NX, NZ = 4, 8
CORES = 2
NCR = 2
FBD = 8
SLOT = 4
BS = 64
VMEM = 63 << 20
CHUNKS = 2
PART = BS // (2 * CHUNKS)


class Geometry:
    def __init__(self, rows, cols, x=NX, z=NZ, slot=SLOT):
        self.rows, self.cols, self.x, self.z, self.slot = rows, cols, x, z, slot
        self.y = rows // CORES
        self.span = rows // slot
        self.pair = z // self.span
        self.n_y, self.n_z = cols, rows * x
        self.out_y = [slot * PART + (8 if ch == 0 else 0) for ch in range(CHUNKS)]
        self.out_z = [self.pair * PART for _ in range(CHUNKS)]


def half_ring(n):
    return n // 2, n - 1 - n // 2


def split(value):
    high = value.astype(BF16)
    return high, (value - high.astype(F32)).astype(BF16)


def dot_t(left, right):
    return lax.dot_general(left, right, (((0,), (0,)), ((), ())), preferred_element_type=F32)


class Ring:
    def __init__(self, steps, sign, send, recv, make):
        self.steps, self.sign, self.send, self.recv, self.make = steps, sign, send, recv, make

    def copy(self, t):
        return self.make(t, self.sign, self.send.at[t - 1], self.recv.at[t - 1])


def fetch_kernel(g, fl_ref, cols_hbm, p_hbm, *refs):
    gy_refs, gz_refs, st_y, st_z, pan_y, pan_z = (refs[n * CHUNKS:(n + 1) * CHUNKS] for n in range(6))
    (
        pay_y, pay_z, tab, smem_y, smem_z, cols,
        up_s, up_r, down_s, down_r, zup_s, zup_r, zdown_s, zdown_r, sib_s, sib_r, tab_s, tab_r, ex_s, ex_r, loc,
    ) = refs[6 * CHUNKS:]
    me_r, me_c = lax.axis_index("row"), lax.axis_index("col")
    y, core = me_r // CORES, me_r % CORES
    x, z = me_c // g.z, me_c % g.z

    def remote(src, dst, send, recv, device):
        return pltpu.make_async_remote_copy(
            src_ref=src, dst_ref=dst, send_sem=send, recv_sem=recv, device_id=device, device_id_type=MESH
        )

    def row_of(yy):
        return ((yy + g.y) % g.y) * CORES + core

    def col_of(xx, zz):
        return ((xx + g.x) % g.x) * g.z + (zz + g.z) % g.z

    own = []
    for ch in range(CHUNKS):
        top, bottom = ch * PART, (CHUNKS + ch) * PART
        own.append(pltpu.make_async_copy(
            p_hbm.at[:, pl.ds(top, PART), :], pan_y[ch].at[pl.ds(me_r * FBD, FBD)], loc.at[2 * ch]))
        own.append(pltpu.make_async_copy(
            p_hbm.at[:, pl.ds(bottom, PART), :], pan_z[ch].at[pl.ds(z * FBD, FBD)], loc.at[2 * ch + 1]))
    base = 2 * CHUNKS
    tag_in = pltpu.make_async_copy(cols_hbm, cols, loc.at[base])

    barrier = pltpu.get_barrier_semaphore()
    near = [(row_of(y + 1), me_c), (row_of(y - 1), me_c), (y * CORES + (1 - core), me_c)]
    near += [(me_r, col_of(x, z + 1)), (me_r, col_of(x, z - 1))]
    near += [(me_r, col_of(x + dx, z)) for dx in range(1, g.x)]
    for device in near:
        pl.semaphore_signal(barrier, inc=1, device_id=device, device_id_type=MESH)
    for copy in own + [tag_in]:
        copy.start()
    table = jnp.concatenate([fl_ref[s:s + 1, :] for s in range(g.slot)], axis=1)
    if table.shape[1] < 128:
        table = jnp.pad(table, ((0, 0), (0, 128 - table.shape[1])))
    tab[0] = table
    tag_in.wait()
    lane = lax.broadcasted_iota(jnp.int32, (1, 128), 1) // BS
    pay_y[me_r, 0:8, :] = jnp.zeros((8, 128), jnp.int32)
    pay_z[z] = jnp.zeros((8, 128), jnp.int32)
    for j in range(FBD):
        pay_y[me_r, 8 + j:9 + j, :] = jnp.where(lane == 0, cols[0, j], cols[1, j])
    for copy in own:
        copy.wait()
    pl.semaphore_wait(barrier, len(near))

    def rings_of(buf_y, buf_z, unit):
        def make_y(t, sign, send, recv):
            view = buf_y.at[pl.ds(row_of(y - sign * (t - 1)) * unit, unit)]
            return remote(view, view, send, recv, (row_of(y + sign), me_c))

        def make_z(t, sign, send, recv):
            view = buf_z.at[pl.ds((z - sign * (t - 1) + g.z) % g.z * unit, unit)]
            return remote(view, view, send, recv, (me_r, col_of(x, z + sign)))

        return make_y, make_z

    class Gather:
        def __init__(self, which, buf_y, buf_z, unit):
            make_y, make_z = rings_of(buf_y, buf_z, unit)
            (up_y, down_y), (up_z, down_z) = (half_ring(n)[::-1 if which % 2 else 1] for n in (g.y, g.z))
            self.y_rings = [
                Ring(up_y, 1, up_s.at[which], up_r.at[which], make_y),
                Ring(down_y, -1, down_s.at[which], down_r.at[which], make_y),
            ]
            self.z_rings = [
                Ring(up_z, 1, zup_s.at[which], zup_r.at[which], make_z),
                Ring(down_z, -1, zdown_s.at[which], zdown_r.at[which], make_z),
            ]
            self.rings = [self.y_rings[0], self.z_rings[0], self.y_rings[1], self.z_rings[1]]
            self.which, self.buf, self.unit, self.sibs = which, buf_y, unit, []

        def sibling(self, yy):
            n = len(self.sibs)
            view = self.buf.at[pl.ds(row_of(yy) * self.unit, self.unit)]
            copy = remote(
                view, view, sib_s.at[self.which, n], sib_r.at[self.which, n], (y * CORES + (1 - core), me_c))
            copy.start()
            self.sibs.append(copy)

        def begin(self):
            for ring in self.rings:
                if ring.steps:
                    ring.copy(1).start()
            self.sibling(y)

        def advance(self, t):
            for ring in self.rings:
                if t <= ring.steps:
                    ring.copy(t).wait_recv()
                    if t < ring.steps:
                        ring.copy(t + 1).start()
                    if ring in self.y_rings:
                        self.sibling(y - ring.sign * t)

        def finish(self):
            for copy in self.sibs:
                copy.wait_recv()

        def drain(self):
            for ring in self.rings:
                for t in range(1, ring.steps + 1):
                    ring.copy(t).wait_send()
            for copy in self.sibs:
                copy.wait_send()

    gathers = [Gather(ch, pan_y[ch], pan_z[ch], FBD) for ch in range(CHUNKS)]
    lists = Gather(CHUNKS, pay_y, pay_z, 1)
    steps = max(g.y, g.z) // 2

    for dx in range(1, g.x):
        remote(tab.at[0], tab.at[dx], tab_s.at[dx - 1], tab_r.at[dx - 1], (me_r, col_of(x + dx, z))).start()
    gathers[0].begin()
    for dx in range(g.x):
        if dx:
            remote(tab.at[0], tab.at[dx], tab_s.at[dx - 1], tab_r.at[dx - 1], (me_r, col_of(x + dx, z))).wait_recv()
        pay_y[me_r, dx:dx + 1, :] = tab[dx]
        pay_z[z, dx:dx + 1, :] = tab[dx]
    lists.begin()
    for ch in range(1, CHUNKS):
        gathers[ch].begin()
    to_smem = [
        pltpu.make_async_copy(pay_z, smem_y, loc.at[base + 1]),
        pltpu.make_async_copy(pay_y.at[:, 0:8, :], smem_z, loc.at[base + 2]),
    ]
    for t in range(1, steps + 1):
        lists.advance(t)
        if t == steps:
            lists.finish()
            for copy in to_smem:
                copy.start()
        gathers[0].advance(t)
        for ch in range(1, CHUNKS):
            if t < steps:
                gathers[ch].advance(t)
    gathers[0].finish()
    for copy in to_smem:
        copy.wait()

    eight = lax.broadcasted_iota(jnp.int32, (8, 128), 0)

    def send_y(ch, t, away):
        dx, dz = t // g.z, t % g.z
        from_z, from_x = (z + dz) % g.z, (g.x - dx) % g.x
        for s in range(g.slot):
            block = smem_y[from_z, from_x, s * g.cols + me_c]
            owner_row, inside = block // (FBD * g.cols), block % FBD
            st_y[ch][t, s * PART:(s + 1) * PART, :] = pan_y[ch][owner_row * FBD + inside]
            if ch == 0:
                tags = jnp.where(eight == inside, pay_y[owner_row, 8:16, :], 0).astype(F32)
                tag = jnp.sum(tags, axis=0, keepdims=True)
                for rep in range(8 // g.slot):
                    row = g.slot * PART + rep * g.slot + s
                    st_y[ch][t, row:row + 1, :] = tag
        if away:
            device = (me_r, col_of(x + dx, z + dz))
            remote(st_y[ch].at[t], gy_refs[ch].at[t], ex_s.at[0, ch], ex_r.at[0, ch], device).start()

    def send_z(ch, t, away):
        dr, dx = t // g.x, t % g.x
        to_row, from_x = (me_r + dr) % g.rows, (g.x - dx) % g.x
        first = smem_z[to_row, from_x, 0] // (FBD * g.cols)
        turn = (me_r - first + g.rows) % g.rows
        s, zz = turn % g.slot, turn // g.slot
        for j in range(g.pair):
            at = zz + g.span * j
            block = smem_z[to_row, from_x, s * g.cols + x * g.z + at]
            st_z[ch][t, j * PART:(j + 1) * PART, :] = pan_z[ch][at * FBD + block % FBD]
        if away:
            device = (to_row, col_of(x + dx, z))
            remote(st_z[ch].at[t], gz_refs[ch].at[t], ex_s.at[1, ch], ex_r.at[1, ch], device).start()

    ratio = g.n_z // g.n_y
    last = []
    for ch in range(CHUNKS):
        for j in range(1, ratio):
            send_z(ch, (j * 29) % g.n_z, True)

        @pl.loop(1, g.n_y)
        def _(q):
            send_y(ch, (q * 13) % g.n_y, True)
            for j in range(ratio):
                send_z(ch, ((ratio * q + j) * 29) % g.n_z, True)

        send_y(ch, 0, False)
        send_z(ch, 0, False)
        for which, (src, dst) in enumerate(((st_y, gy_refs), (st_z, gz_refs))):
            copy = pltpu.make_async_copy(src[ch].at[0], dst[ch].at[0], loc.at[base + 3 + 2 * ch + which])
            copy.start()
            last.append(copy)
        if ch + 1 < CHUNKS:
            gathers[ch + 1].advance(steps)
            gathers[ch + 1].finish()

    for copy in last:
        copy.wait()
    for dx in range(1, g.x):
        remote(tab.at[0], tab.at[dx], tab_s.at[dx - 1], tab_r.at[dx - 1], (me_r, col_of(x + dx, z))).wait_send()
    lists.drain()
    for gather in gathers:
        gather.drain()
    for ch in range(CHUNKS):
        for which, (src, dst, n) in enumerate(((st_y, gy_refs, g.n_y), (st_z, gz_refs, g.n_z))):
            view_s, view_d = src[ch].at[pl.ds(1, n - 1)], dst[ch].at[pl.ds(1, n - 1)]
            rest = remote(view_s, view_d, ex_s.at[which, ch], ex_r.at[which, ch], (me_r, col_of(x, z + 1)))
            rest.wait_send()
            rest.wait_recv()


def fetch(g, requests, cols, prolong_blocks):
    far_y, far_z = max(half_ring(g.y)), max(half_ring(g.z))
    dma = pltpu.SemaphoreType.DMA
    hbm = pl.BlockSpec(memory_space=pltpu.HBM)
    got = [jax.ShapeDtypeStruct((g.n_y, n, 128), F32) for n in g.out_y]
    got += [jax.ShapeDtypeStruct((g.n_z, n, 128), F32) for n in g.out_z]
    kinds = CHUNKS + 1
    return pl.pallas_call(
        functools.partial(fetch_kernel, g),
        out_shape=tuple(got),
        in_specs=[pl.BlockSpec(memory_space=pltpu.VMEM), hbm, hbm],
        out_specs=(hbm,) * (2 * CHUNKS),
        scratch_shapes=[
            *[pltpu.VMEM(s.shape, F32) for s in got],
            *[pltpu.VMEM((g.rows * FBD, PART, 128), F32) for _ in range(CHUNKS)],
            *[pltpu.VMEM((g.z * FBD, PART, 128), F32) for _ in range(CHUNKS)],
            pltpu.VMEM((g.rows, 16, 128), jnp.int32),
            pltpu.VMEM((g.z, 8, 128), jnp.int32),
            pltpu.VMEM((g.x, 1, 128), jnp.int32),
            pltpu.SMEM((g.z, 8, 128), jnp.int32),
            pltpu.SMEM((g.rows, 8, 128), jnp.int32),
            pltpu.SMEM(cols.shape, jnp.int32),
            dma((kinds, far_y)), dma((kinds, far_y)), dma((kinds, far_y)), dma((kinds, far_y)),
            dma((kinds, far_z)), dma((kinds, far_z)), dma((kinds, far_z)), dma((kinds, far_z)),
            dma((kinds, g.y)), dma((kinds, g.y)),
            dma((max(g.x - 1, 1),)), dma((max(g.x - 1, 1),)),
            dma((2, CHUNKS)), dma((2, CHUNKS)), dma((4 * CHUNKS + 3,)),
        ],
        compiler_params=pltpu.CompilerParams(
            collective_id=0, has_side_effects=True, vmem_limit_bytes=VMEM
        ),
        name="fetch",
    )(requests, cols, prolong_blocks)


def product_kernel(g, n_i, n_k, fetch_hbm, slot_hbm, count_hbm, rows_hbm, a_hbm, r_hbm, *refs):
    got_hbm, refs = refs[:2 * CHUNKS], refs[2 * CHUNKS:]
    acc_ref, got, refs = refs[0], refs[1:1 + 2 * CHUNKS], refs[1 + 2 * CHUNKS:]
    w, a_ref, r_ref, requests, slots, count, rows, tags, sem, a_sem = refs
    me_r, me_c = lax.axis_index("row"), lax.axis_index("col")
    x, z = me_c // g.z, me_c % g.z
    early = [
        pltpu.make_async_copy(rows_hbm, rows, sem.at[0]),
        pltpu.make_async_copy(count_hbm, count, sem.at[1]),
        pltpu.make_async_copy(r_hbm, r_ref, sem.at[2]),
    ]
    late = [
        pltpu.make_async_copy(slot_hbm, slots, sem.at[3]),
        pltpu.make_async_copy(fetch_hbm, requests, sem.at[4]),
        pltpu.make_async_copy(got_hbm[0].at[:, pl.ds(g.slot * PART, 8), :], tags, sem.at[5]),
    ]
    late += [pltpu.make_async_copy(src, dst, sem.at[6 + n]) for n, (src, dst) in enumerate(zip(got_hbm, got))]

    def block_row(i):
        return pltpu.make_async_copy(a_hbm.at[i], a_ref.at[i], a_sem.at[i])

    for copy in early:
        copy.start()
    for i in range(n_i):
        block_row(i).start()
    for copy in late:
        copy.start()
    acc_ref[...] = jnp.zeros_like(acc_ref)
    half = lax.broadcasted_iota(jnp.int32, (BS, 2 * BS), 1) // BS
    for copy in early:
        copy.wait()

    @pl.loop(0, n_i)
    def _(i):
        block_row(i).wait()
        stored = r_ref[i]
        swapped = pltpu.roll(stored, BS, 1)
        first, second = rows[0, i], rows[1, i]
        mine = jnp.where(half == 0, first, second)
        other = jnp.where(half == 0, second, first)
        dense = jnp.where(mine == half, stored, 0.0) + jnp.where(other == half, swapped, 0.0)
        r_hi, r_lo = split(dense)
        a_hi, a_lo = split(a_ref[i])
        ra = dot_t(
            jnp.concatenate([a_hi, a_lo, a_hi], axis=0),
            jnp.concatenate([r_hi, r_hi, r_lo], axis=0),
        )
        for k in range(n_k):
            part = jnp.where(k < count[i], ra[k * BS:(k + 1) * BS, :], 0.0)
            hi, lo = split(part)
            w[i * n_k + k, 0:BS, :] = hi
            w[i * n_k + k, BS:2 * BS, :] = lo

    for copy in late:
        copy.wait()

    @pl.loop(0, n_i)
    def _(i):
        for k in range(n_k):
            slot = slots[i, k]
            peer, s = slot // g.slot, slot % g.slot
            px, pz = peer // g.z, peer % g.z
            owner_row = requests[s, peer] // (FBD * g.cols)
            dx = (x - px + g.x) % g.x
            t = dx * g.z + (z - pz + g.z) % g.z
            tz = ((me_r - owner_row + g.rows) % g.rows) * g.x + dx
            j = pz // g.span
            top = [got[ch][t, pl.ds(pl.multiple_of(s * PART, 8), PART), :] for ch in range(CHUNKS)]
            bottom = [got[CHUNKS + ch][tz, pl.ds(pl.multiple_of(j * PART, 8), PART), :] for ch in range(CHUNKS)]
            p_hi, p_lo = split(jnp.concatenate(top + bottom, axis=0))
            w_hi, w_lo = w[i * n_k + k, 0:BS, :], w[i * n_k + k, BS:2 * BS, :]
            out = dot_t(jnp.concatenate([p_hi, p_lo, p_hi], axis=0), jnp.concatenate([w_hi, w_hi, w_lo], axis=0))
            first = tags[t, s, 0].astype(jnp.int32)
            second = tags[t, s, BS].astype(jnp.int32)
            acc_ref[first] += out[0:BS, :]
            acc_ref[second] += out[BS:2 * BS, :]


def product(g, requests, slots, counts, rows, blocks, restrict, got):
    n_i, n_k = slots.shape
    hbm = pl.BlockSpec(memory_space=pltpu.HBM)
    return pl.pallas_call(
        functools.partial(product_kernel, g, n_i, n_k),
        out_shape=jax.ShapeDtypeStruct((NCR * g.rows, BS, NCR * BS), F32),
        in_specs=[hbm] * (6 + 2 * CHUNKS),
        out_specs=pl.BlockSpec(memory_space=pltpu.VMEM),
        scratch_shapes=[
            *[pltpu.VMEM(a.shape, F32) for a in got],
            pltpu.VMEM((n_i * n_k, 2 * BS, NCR * BS), BF16),
            pltpu.VMEM(blocks.shape, F32),
            pltpu.VMEM(restrict.shape, F32),
            pltpu.SMEM(requests.shape, jnp.int32),
            pltpu.SMEM(slots.shape, jnp.int32),
            pltpu.SMEM(counts.shape, jnp.int32),
            pltpu.SMEM(rows.shape, jnp.int32),
            pltpu.SMEM((g.cols, 8, 128), F32),
            pltpu.SemaphoreType.DMA((6 + 2 * CHUNKS,)),
            pltpu.SemaphoreType.DMA((n_i,)),
        ],
        compiler_params=pltpu.CompilerParams(vmem_limit_bytes=VMEM),
        name="product",
    )(requests, slots, counts, rows, blocks, restrict, *got)


def reduce_kernel(g, acc_ref, o_ref, r1, s1, r2, s1_send, s1_recv, s2_send, s2_recv):
    me_r, me_c = lax.axis_index("row"), lax.axis_index("col")
    x, z = me_c // g.z, me_c % g.z
    per = acc_ref.shape[0] // g.cols
    barrier = pltpu.get_barrier_semaphore()

    def col_x(dx):
        return ((x + dx) % g.x) * g.z + z

    def col_z(dz):
        return x * g.z + (z + dz) % g.z

    for dx in range(1, g.x):
        pl.semaphore_signal(barrier, inc=1, device_id=(me_r, col_x(dx)), device_id_type=MESH)
    for dz in range(1, g.z):
        pl.semaphore_signal(barrier, inc=1, device_id=(me_r, col_z(dz)), device_id_type=MESH)
    pl.semaphore_wait(barrier, g.x + g.z - 2)

    order = sorted(range(g.z), key=lambda dz: -min(dz, g.z - dz))
    first = []
    for dz in order:
        for dx in range(1, g.x):
            tile = ((x + dx) % g.x) * g.z + (z + dz) % g.z
            copy = pltpu.make_async_remote_copy(
                src_ref=acc_ref.at[pl.ds(tile * per, per)], dst_ref=r1.at[dz, dx - 1],
                send_sem=s1_send.at[dz, dx - 1], recv_sem=s1_recv.at[dz, dx - 1],
                device_id=(me_r, col_x(dx)), device_id_type=MESH,
            )
            copy.start()
            first.append((dz, copy))
    second = []
    for dz in order:
        for at, copy in first:
            if at == dz:
                copy.wait_recv()
        tile = x * g.z + (z + dz) % g.z
        total = acc_ref[pl.ds(tile * per, per)]
        for dx in range(1, g.x):
            total = total + r1[dz, dx - 1]
        s1[dz] = total
        if dz:
            copy = pltpu.make_async_remote_copy(
                src_ref=s1.at[dz], dst_ref=r2.at[dz - 1],
                send_sem=s2_send.at[dz - 1], recv_sem=s2_recv.at[dz - 1],
                device_id=(me_r, col_z(dz)), device_id_type=MESH,
            )
            copy.start()
            second.append((dz, copy))
    total = s1[0]
    for dz, copy in second:
        copy.wait_recv()
        total = total + r2[dz - 1]
    o_ref[...] = total
    for _, copy in first + second:
        copy.wait_send()


def reduce(g, acc):
    tile = acc.shape[1:]
    per = acc.shape[0] // g.cols
    vmem = pl.BlockSpec(memory_space=pltpu.VMEM)
    dma = pltpu.SemaphoreType.DMA
    return pl.pallas_call(
        functools.partial(reduce_kernel, g),
        out_shape=jax.ShapeDtypeStruct((per,) + tile, F32),
        in_specs=[vmem],
        out_specs=vmem,
        scratch_shapes=[
            pltpu.VMEM((g.z, max(g.x - 1, 1), per) + tile, F32),
            pltpu.VMEM((g.z, per) + tile, F32),
            pltpu.VMEM((g.z - 1, per) + tile, F32),
            dma((g.z, max(g.x - 1, 1))), dma((g.z, max(g.x - 1, 1))),
            dma((g.z - 1,)), dma((g.z - 1,)),
        ],
        compiler_params=pltpu.CompilerParams(collective_id=1, has_side_effects=True),
        name="reduce",
    )(acc)


def local(
    g,
    operator_blocks,
    operator_count,
    operator_slot,
    fetch_lists,
    prolong_blocks,
    prolong_cols,
    restrict_blocks,
    restrict_rows,
):
    requests = fetch_lists.reshape(g.cols, g.slot).T
    got = fetch(g, requests, prolong_cols.T, prolong_blocks)
    acc = product(
        g, requests, operator_slot, operator_count, restrict_rows.T, operator_blocks, restrict_blocks, got
    )
    share = reduce(g, acc)
    return share.reshape(-1, NCR * BS).T


def solution(mesh):
    g = Geometry(mesh.shape["row"], mesh.shape["col"])
    return jax.shard_map(
        functools.partial(local, g),
        mesh=mesh,
        in_specs=(
            P(("row", "col"), None, None),
            P(("row", "col")),
            P(("row", "col"), None),
            P("row", "col", None, None),
            P(("row", "col"), None, None),
            P(("row", "col"), None),
            P(("row", "col"), None, None),
            P(("row", "col"), None),
        ),
        out_specs=P("row", "col"),
        check_vma=False,
    )
```

time: 433 us -> 118 us (0.27)
  waiting for transfers between devices: 309 us -> 0 us
  Pallas kernels: 0 us -> 116 us
  starting transfers between devices: 33.9 us -> 0 us
  matrix products: 26.8 us -> 0 us
  local copies, waits for them, and re-layouts: 25.8 us -> 1.38 us
  blocking collectives: 18.6 us -> 0 us
  between operations: 13.5 us -> 0.02 us
    unnamed x3 -> x0, waiting for transfers between devices: 212 us -> none
    pallas_call x0 -> x3, Pallas kernels: none -> 116 us  [the longest x1 86.4 us: fetch(): pl.pallas_call(functools.partial(fetch_kernel, g), out_shape=tuple(got),...]
    all_to_all x3 -> x0, waiting for transfers between devices: 89.6 us -> none  [the longest x1 89.6 us: local(): lax.all_to_all(fetched, 'col', split_axis=0, concat_axis=0, tiled=True)]
    all_to_all x3 -> x0, starting transfers between devices: 33.6 us -> none  [the longest x1 13.7 us: local(): lax.all_to_all(requests, 'col', split_axis=0, concat_axis=0, tiled=True)]
    dot_general x4 -> x0, matrix products: 26.8 us -> none  [contract(): return jnp.einsum(form, left, right, precision=lax.Precision.HIGHEST)]
    all_gather x1 -> x0, blocking collectives: 18.6 us -> none  [gather_panel(): lax.all_gather(prolong_cols, 'row', axis=0, tiled=True)]
    gather x6 -> x0, local copies, waits for them, and re-layouts: 10.1 us -> none  [the longest x1 4.95 us: local(): fetched = panel_blocks[position]]
    reshape x3 -> x0, local copies, waits for them, and re-layouts: 7.75 us -> none  [the longest x1 5.63 us: local(): products.reshape(fine_rows, row_entries, block_size, prolong_entries, blo...]
  transfers between devices with their start and end apart: 5 -> 0, of which waited for: 3 -> 0; matrix products, arithmetic and copies ran while one was open for 3% -> 0% of each run, Pallas kernels for 0% -> 0%
where the time goes in v3:
time: 118 us; the launch traced here: 117 us
  Pallas kernels  116 us (98%)
  local copies, waits for them, and re-layouts  1.38 us (1%)
    pallas_call x1, Pallas kernels, fetch(): pl.pallas_call(functools.partial(fetch_kernel, g), out_shape=tuple(got),...  86.4 us
    pallas_call x1, Pallas kernels, reduce(): pl.pallas_call(functools.partial(reduce_kernel, g), out_shape=jax.ShapeDt...  20.8 us
    pallas_call x1, Pallas kernels, product(): pl.pallas_call(functools.partial(product_kernel, g, n_i, n_k), out_shape=...  8.74 us

profile of v3, /device:TPU:1, one launch (start us, length us, event | category | flops | bytes accessed | tf_op | source)
XLA Modules:
  0.0 117.4 jit_solution(1619343834544035381)
XLA Ops:
  0.0 86.4 %fetch.1 = (f32[32,72,128]{2,1,0:T(8,128)}, f32[32,64,128]{2,1,0:T(8,128)}, f32[64,32,128]{2,1,0:T(8,128)}, f32[64,32,128]{2,1,0:T(8,128)}) custom-call(s32[4,32]{1,0:T(4,128)} %bitcast.9, s32[2,8]{1,0:T(2,128)} %bitcast.11, f32[8,64,128]{2,1,0:T(8,128)} %p_hbm.1), custom_call_target="tpu_custom_call" | custom-call | tf_op jit(solution)/shard_map/fetch/pallas_call | solution.py:280
  86.4 8.7 %product.1.acc_ref = f32[32,64,128]{2,1,0:T(8,128)} custom-call(s32[4,32]{1,0:T(4,128)} %bitcast.10, s32[8,8]{1,0:T(8,128)} %slot_hbm.1, s32[8]{0:T(128)} %count_hbm.1, s32[2,8]{1,0:T(2,128)} %bitcast.12, f32[8,64,512]{2,1,0:T(8,128)} %a_hbm.1, f32[8,64,128]{2,1,0:T(8,128)} %r_hbm.1, f32[32,72,128]{2,1,0:T(8,128)} %get-tuple-element.9.refs_0_, ...), custom_call_target="tpu_custom_call" | custom-call | tf_op jit(solution)/shard_map/product/pallas_call | solution.py:389
  95.2 20.8 %reduce.1 = f32[1,64,128]{2,1,0:T(8,128)} custom-call(f32[32,64,128]{2,1,0:T(8,128)} %product.1.acc_ref), custom_call_target="tpu_custom_call" | custom-call | tf_op jit(solution)/shard_map/reduce/pallas_call | solution.py:474
  116.0 1.4 %copy.10 = f32[128,64]{0,1:T(8,128)} copy(f32[128,64]{0,1:T(8,128)} %bitcast.8) | data formatting | bytes 65536

commit v4 on v3

--- a/solution.py
+++ b/solution.py
@@ -409,81 +409,93 @@
     )(requests, slots, counts, rows, blocks, restrict, *got)
 
 
-def reduce_kernel(g, acc_ref, o_ref, r1, s1, r2, s1_send, s1_recv, s2_send, s2_recv):
+def reduce_kernel(g, acc_hbm, o_ref, acc, far, near, relay, relayed, s1, r2, sems, load, s2_send, s2_recv):
     me_r, me_c = lax.axis_index("row"), lax.axis_index("col")
     x, z = me_c // g.z, me_c % g.z
-    per = acc_ref.shape[0] // g.cols
+    half = BS // 2
+    load_acc = pltpu.make_async_copy(acc_hbm, acc, load.at[0])
+    load_acc.start()
     barrier = pltpu.get_barrier_semaphore()
 
-    def col_x(dx):
-        return ((x + dx) % g.x) * g.z + z
-
-    def col_z(dz):
-        return x * g.z + (z + dz) % g.z
-
-    for dx in range(1, g.x):
-        pl.semaphore_signal(barrier, inc=1, device_id=(me_r, col_x(dx)), device_id_type=MESH)
-    for dz in range(1, g.z):
-        pl.semaphore_signal(barrier, inc=1, device_id=(me_r, col_z(dz)), device_id_type=MESH)
-    pl.semaphore_wait(barrier, g.x + g.z - 2)
+    def at_x(dx):
+        return (me_r, ((x + dx) % g.x) * g.z + z)
+
+    def at_z(dz):
+        return (me_r, x * g.z + (z + dz) % g.z)
+
+    for device in [at_x(1), at_x(3)] + [at_z(dz) for dz in range(1, g.z)]:
+        pl.semaphore_signal(barrier, inc=1, device_id=device, device_id_type=MESH)
+    pl.semaphore_wait(barrier, g.z + 1)
+    load_acc.wait()
+
+    def tile(dx, dz):
+        return ((x + dx) % g.x) * g.z + (z + dz) % g.z
+
+    def send(kind, way, dz, src, dst):
+        copy = pltpu.make_async_remote_copy(
+            src_ref=src, dst_ref=dst.at[way, dz],
+            send_sem=sems.at[kind, way, dz, 0], recv_sem=sems.at[kind, way, dz, 1],
+            device_id=at_x(1 if way == 0 else 3), device_id_type=MESH,
+        )
+        copy.start()
+        return copy
 
     order = sorted(range(g.z), key=lambda dz: -min(dz, g.z - dz))
-    first = []
+    rows = (pl.ds(0, half), pl.ds(half, half))
+    fars, nears, relays, lasts = {}, {}, {}, {}
     for dz in order:
-        for dx in range(1, g.x):
-            tile = ((x + dx) % g.x) * g.z + (z + dz) % g.z
-            copy = pltpu.make_async_remote_copy(
-                src_ref=acc_ref.at[pl.ds(tile * per, per)], dst_ref=r1.at[dz, dx - 1],
-                send_sem=s1_send.at[dz, dx - 1], recv_sem=s1_recv.at[dz, dx - 1],
-                device_id=(me_r, col_x(dx)), device_id_type=MESH,
-            )
-            copy.start()
-            first.append((dz, copy))
-    second = []
+        for way in range(2):
+            fars[way, dz] = send(0, way, dz, acc.at[tile(2, dz), rows[way], :], far)
     for dz in order:
-        for at, copy in first:
-            if at == dz:
-                copy.wait_recv()
-        tile = x * g.z + (z + dz) % g.z
-        total = acc_ref[pl.ds(tile * per, per)]
-        for dx in range(1, g.x):
-            total = total + r1[dz, dx - 1]
-        s1[dz] = total
+        for way in range(2):
+            step = 1 if way == 0 else 3
+            nears[way, dz] = send(1, way, dz, acc.at[tile(step, dz), rows[1 - way], :], near)
+        for way in range(2):
+            step = 1 if way == 0 else 3
+            fars[way, dz].wait_recv()
+            relay[way, dz] = acc[tile(step, dz), rows[way], :] + far[way, dz]
+            relays[way, dz] = send(2, way, dz, relay.at[way, dz], relayed)
+    for dz in order:
+        for way in range(2):
+            relays[way, dz].wait_recv()
+            nears[1 - way, dz].wait_recv()
+            s1[dz, rows[way], :] = acc[tile(0, dz), rows[way], :] + relayed[way, dz] + near[1 - way, dz]
         if dz:
-            copy = pltpu.make_async_remote_copy(
+            lasts[dz] = pltpu.make_async_remote_copy(
                 src_ref=s1.at[dz], dst_ref=r2.at[dz - 1],
                 send_sem=s2_send.at[dz - 1], recv_sem=s2_recv.at[dz - 1],
-                device_id=(me_r, col_z(dz)), device_id_type=MESH,
+                device_id=at_z(dz), device_id_type=MESH,
             )
-            copy.start()
-            second.append((dz, copy))
+            lasts[dz].start()
     total = s1[0]
-    for dz, copy in second:
+    for dz, copy in lasts.items():
         copy.wait_recv()
         total = total + r2[dz - 1]
     o_ref[...] = total
-    for _, copy in first + second:
-        copy.wait_send()
+    for group in (fars, nears, relays, lasts):
+        for copy in group.values():
+            copy.wait_send()
 
 
 def reduce(g, acc):
-    tile = acc.shape[1:]
-    per = acc.shape[0] // g.cols
-    vmem = pl.BlockSpec(memory_space=pltpu.VMEM)
+    rows, lanes = acc.shape[1:]
+    part = pltpu.VMEM((2, g.z, rows // 2, lanes), F32)
     dma = pltpu.SemaphoreType.DMA
     return pl.pallas_call(
         functools.partial(reduce_kernel, g),
-        out_shape=jax.ShapeDtypeStruct((per,) + tile, F32),
-        in_specs=[vmem],
-        out_specs=vmem,
+        out_shape=jax.ShapeDtypeStruct((rows, lanes), F32),
+        in_specs=[pl.BlockSpec(memory_space=pltpu.HBM)],
+        out_specs=pl.BlockSpec(memory_space=pltpu.VMEM),
         scratch_shapes=[
-            pltpu.VMEM((g.z, max(g.x - 1, 1), per) + tile, F32),
-            pltpu.VMEM((g.z, per) + tile, F32),
-            pltpu.VMEM((g.z - 1, per) + tile, F32),
-            dma((g.z, max(g.x - 1, 1))), dma((g.z, max(g.x - 1, 1))),
-            dma((g.z - 1,)), dma((g.z - 1,)),
+            pltpu.VMEM(acc.shape, F32),
+            part, part, part, part,
+            pltpu.VMEM((g.z, rows, lanes), F32),
+            pltpu.VMEM((g.z - 1, rows, lanes), F32),
+            dma((3, 2, g.z, 2)), dma((1,)), dma((g.z - 1,)), dma((g.z - 1,)),
         ],
-        compiler_params=pltpu.CompilerParams(collective_id=1, has_side_effects=True),
+        compiler_params=pltpu.CompilerParams(
+            collective_id=1, has_side_effects=True, vmem_limit_bytes=VMEM
+        ),
         name="reduce",
     )(acc)
 
@@ -505,7 +517,7 @@
         g, requests, operator_slot, operator_count, restrict_rows.T, operator_blocks, restrict_blocks, got
     )
     share = reduce(g, acc)
-    return share.reshape(-1, NCR * BS).T
+    return share.T
 
 
 def solution(mesh):

time: 118 us -> 116 us (0.983); the launches traced: 117 us -> 114 us
  Pallas kernels: 116 us -> 112 us
    pallas_call x1, Pallas kernels: 20.8 us -> 17.2 us  [reduce(): pl.pallas_call(functools.partial(reduce_kernel, g), out_shape=jax.ShapeDt...]
where the time goes in v4:
time: 116 us; the launch traced here: 114 us
  Pallas kernels  112 us (97%)
  local copies, waits for them, and re-layouts  1.38 us (1%)
    pallas_call x1, Pallas kernels, fetch(): pl.pallas_call(functools.partial(fetch_kernel, g), out_shape=tuple(got),...  86.4 us
    pallas_call x1, Pallas kernels, reduce(): pl.pallas_call(functools.partial(reduce_kernel, g), out_shape=jax.ShapeDt...  17.2 us
    pallas_call x1, Pallas kernels, product(): pl.pallas_call(functools.partial(product_kernel, g, n_i, n_k), out_shape=...  8.74 us

profile of v4, /device:TPU:1, one launch (start us, length us, event | category | flops | bytes accessed | tf_op | source)
XLA Modules:
  0.0 113.7 jit_solution(3090917611434060526)
XLA Ops:
  0.0 86.4 %fetch.1 = (f32[32,72,128]{2,1,0:T(8,128)}, f32[32,64,128]{2,1,0:T(8,128)}, f32[64,32,128]{2,1,0:T(8,128)}, f32[64,32,128]{2,1,0:T(8,128)}) custom-call(s32[4,32]{1,0:T(4,128)} %bitcast.7, s32[2,8]{1,0:T(2,128)} %bitcast.9, f32[8,64,128]{2,1,0:T(8,128)} %p_hbm.1), custom_call_target="tpu_custom_call" | custom-call | tf_op jit(solution)/shard_map/fetch/pallas_call | solution.py:280
  86.4 8.7 %product.1.acc_hbm = f32[32,64,128]{2,1,0:T(8,128)} custom-call(s32[4,32]{1,0:T(4,128)} %bitcast.8, s32[8,8]{1,0:T(8,128)} %slot_hbm.1, s32[8]{0:T(128)} %count_hbm.1, s32[2,8]{1,0:T(2,128)} %bitcast.10, f32[8,64,512]{2,1,0:T(8,128)} %a_hbm.1, f32[8,64,128]{2,1,0:T(8,128)} %r_hbm.1, f32[32,72,128]{2,1,0:T(8,128)} %get-tuple-element.9.refs_0_, ...), custom_call_target="tpu_custom_call" | custom-call | tf_op jit(solution)/shard_map/product/pallas_call | solution.py:389
  95.2 17.2 %reduce.1 = f32[64,128]{1,0:T(8,128)} custom-call(f32[32,64,128]{2,1,0:T(8,128)} %product.1.acc_hbm), custom_call_target="tpu_custom_call" | custom-call | tf_op jit(solution)/shard_map/reduce/pallas_call | solution.py:484
  112.3 1.4 %copy.10 = f32[128,64]{0,1:T(8,128)} copy(f32[128,64]{0,1:T(8,128)} %bitcast.6) | data formatting | bytes 65536

commit v5 on v4

--- a/solution.py
+++ b/solution.py
@@ -29,7 +29,7 @@
         self.span = rows // slot
         self.pair = z // self.span
         self.n_y, self.n_z = cols, rows * x
-        self.out_y = [slot * PART + (8 if ch == 0 else 0) for ch in range(CHUNKS)]
+        self.out_y = [slot * PART for _ in range(CHUNKS)]
         self.out_z = [self.pair * PART for _ in range(CHUNKS)]
 
 
@@ -54,10 +54,10 @@
         return self.make(t, self.sign, self.send.at[t - 1], self.recv.at[t - 1])
 
 
-def fetch_kernel(g, fl_ref, cols_hbm, p_hbm, *refs):
+def fetch_kernel(g, fl_ref, cols_hbm, p_hbm, gt_ref, *refs):
     gy_refs, gz_refs, st_y, st_z, pan_y, pan_z = (refs[n * CHUNKS:(n + 1) * CHUNKS] for n in range(6))
     (
-        pay_y, pay_z, tab, smem_y, smem_z, cols,
+        st_t, pay_y, pay_z, tab, smem_y, smem_z, cols,
         up_s, up_r, down_s, down_r, zup_s, zup_r, zdown_s, zdown_r, sib_s, sib_r, tab_s, tab_r, ex_s, ex_r, loc,
     ) = refs[6 * CHUNKS:]
     me_r, me_c = lax.axis_index("row"), lax.axis_index("col")
@@ -201,22 +201,25 @@
         copy.wait()
 
     eight = lax.broadcasted_iota(jnp.int32, (8, 128), 0)
+    place = lax.broadcasted_iota(jnp.int32, (1, 128), 1) % BS // (BS // g.slot)
 
     def send_y(ch, t, away):
         dx, dz = t // g.z, t % g.z
         from_z, from_x = (z + dz) % g.z, (g.x - dx) % g.x
+        row = jnp.zeros((1, 128), F32)
         for s in range(g.slot):
             block = smem_y[from_z, from_x, s * g.cols + me_c]
             owner_row, inside = block // (FBD * g.cols), block % FBD
             st_y[ch][t, s * PART:(s + 1) * PART, :] = pan_y[ch][owner_row * FBD + inside]
             if ch == 0:
                 tags = jnp.where(eight == inside, pay_y[owner_row, 8:16, :], 0).astype(F32)
-                tag = jnp.sum(tags, axis=0, keepdims=True)
-                for rep in range(8 // g.slot):
-                    row = g.slot * PART + rep * g.slot + s
-                    st_y[ch][t, row:row + 1, :] = tag
+                row = jnp.where(place == s, jnp.sum(tags, axis=0, keepdims=True), row)
+        if ch == 0:
+            st_t[t] = row
         if away:
             device = (me_r, col_of(x + dx, z + dz))
+            if ch == 0:
+                remote(st_t.at[t], gt_ref.at[t], ex_s.at[2, 0], ex_r.at[2, 0], device).start()
             remote(st_y[ch].at[t], gy_refs[ch].at[t], ex_s.at[0, ch], ex_r.at[0, ch], device).start()
 
     def send_z(ch, t, away):
@@ -251,6 +254,10 @@
             copy = pltpu.make_async_copy(src[ch].at[0], dst[ch].at[0], loc.at[base + 3 + 2 * ch + which])
             copy.start()
             last.append(copy)
+        if ch == 0:
+            copy = pltpu.make_async_copy(st_t.at[0], gt_ref.at[0], loc.at[base + 3 + 2 * CHUNKS])
+            copy.start()
+            last.append(copy)
         if ch + 1 < CHUNKS:
             gathers[ch + 1].advance(steps)
             gathers[ch + 1].finish()
@@ -262,6 +269,10 @@
     lists.drain()
     for gather in gathers:
         gather.drain()
+    view_s, view_d = st_t.at[pl.ds(1, g.n_y - 1)], gt_ref.at[pl.ds(1, g.n_y - 1)]
+    rest = remote(view_s, view_d, ex_s.at[2, 0], ex_r.at[2, 0], (me_r, col_of(x, z + 1)))
+    rest.wait_send()
+    rest.wait_recv()
     for ch in range(CHUNKS):
         for which, (src, dst, n) in enumerate(((st_y, gy_refs, g.n_y), (st_z, gz_refs, g.n_z))):
             view_s, view_d = src[ch].at[pl.ds(1, n - 1)], dst[ch].at[pl.ds(1, n - 1)]
@@ -279,13 +290,14 @@
     kinds = CHUNKS + 1
     return pl.pallas_call(
         functools.partial(fetch_kernel, g),
-        out_shape=tuple(got),
+        out_shape=(jax.ShapeDtypeStruct((g.n_y, 1, 128), F32), *got),
         in_specs=[pl.BlockSpec(memory_space=pltpu.VMEM), hbm, hbm],
-        out_specs=(hbm,) * (2 * CHUNKS),
+        out_specs=(hbm,) * (2 * CHUNKS + 1),
         scratch_shapes=[
             *[pltpu.VMEM(s.shape, F32) for s in got],
             *[pltpu.VMEM((g.rows * FBD, PART, 128), F32) for _ in range(CHUNKS)],
             *[pltpu.VMEM((g.z * FBD, PART, 128), F32) for _ in range(CHUNKS)],
+            pltpu.VMEM((g.n_y, 1, 128), F32),
             pltpu.VMEM((g.rows, 16, 128), jnp.int32),
             pltpu.VMEM((g.z, 8, 128), jnp.int32),
             pltpu.VMEM((g.x, 1, 128), jnp.int32),
@@ -296,7 +308,7 @@
             dma((kinds, far_z)), dma((kinds, far_z)), dma((kinds, far_z)), dma((kinds, far_z)),
             dma((kinds, g.y)), dma((kinds, g.y)),
             dma((max(g.x - 1, 1),)), dma((max(g.x - 1, 1),)),
-            dma((2, CHUNKS)), dma((2, CHUNKS)), dma((4 * CHUNKS + 3,)),
+            dma((3, CHUNKS)), dma((3, CHUNKS)), dma((4 * CHUNKS + 4,)),
         ],
         compiler_params=pltpu.CompilerParams(
             collective_id=0, has_side_effects=True, vmem_limit_bytes=VMEM
@@ -305,7 +317,7 @@
     )(requests, cols, prolong_blocks)
 
 
-def product_kernel(g, n_i, n_k, fetch_hbm, slot_hbm, count_hbm, rows_hbm, a_hbm, r_hbm, *refs):
+def product_kernel(g, n_i, n_k, fetch_hbm, slot_hbm, count_hbm, rows_hbm, a_hbm, r_hbm, tag_hbm, *refs):
     got_hbm, refs = refs[:2 * CHUNKS], refs[2 * CHUNKS:]
     acc_ref, got, refs = refs[0], refs[1:1 + 2 * CHUNKS], refs[1 + 2 * CHUNKS:]
     w, a_ref, r_ref, requests, slots, count, rows, tags, sem, a_sem = refs
@@ -319,7 +331,7 @@
     late = [
         pltpu.make_async_copy(slot_hbm, slots, sem.at[3]),
         pltpu.make_async_copy(fetch_hbm, requests, sem.at[4]),
-        pltpu.make_async_copy(got_hbm[0].at[:, pl.ds(g.slot * PART, 8), :], tags, sem.at[5]),
+        pltpu.make_async_copy(tag_hbm, tags, sem.at[5]),
     ]
     late += [pltpu.make_async_copy(src, dst, sem.at[6 + n]) for n, (src, dst) in enumerate(zip(got_hbm, got))]
 
@@ -377,19 +389,19 @@
             p_hi, p_lo = split(jnp.concatenate(top + bottom, axis=0))
             w_hi, w_lo = w[i * n_k + k, 0:BS, :], w[i * n_k + k, BS:2 * BS, :]
             out = dot_t(jnp.concatenate([p_hi, p_lo, p_hi], axis=0), jnp.concatenate([w_hi, w_hi, w_lo], axis=0))
-            first = tags[t, s, 0].astype(jnp.int32)
-            second = tags[t, s, BS].astype(jnp.int32)
+            first = tags[t, 0, s * (BS // g.slot)].astype(jnp.int32)
+            second = tags[t, 0, BS + s * (BS // g.slot)].astype(jnp.int32)
             acc_ref[first] += out[0:BS, :]
             acc_ref[second] += out[BS:2 * BS, :]
 
 
-def product(g, requests, slots, counts, rows, blocks, restrict, got):
+def product(g, requests, slots, counts, rows, blocks, restrict, tags, got):
     n_i, n_k = slots.shape
     hbm = pl.BlockSpec(memory_space=pltpu.HBM)
     return pl.pallas_call(
         functools.partial(product_kernel, g, n_i, n_k),
         out_shape=jax.ShapeDtypeStruct((NCR * g.rows, BS, NCR * BS), F32),
-        in_specs=[hbm] * (6 + 2 * CHUNKS),
+        in_specs=[hbm] * (7 + 2 * CHUNKS),
         out_specs=pl.BlockSpec(memory_space=pltpu.VMEM),
         scratch_shapes=[
             *[pltpu.VMEM(a.shape, F32) for a in got],
@@ -400,13 +412,13 @@
             pltpu.SMEM(slots.shape, jnp.int32),
             pltpu.SMEM(counts.shape, jnp.int32),
             pltpu.SMEM(rows.shape, jnp.int32),
-            pltpu.SMEM((g.cols, 8, 128), F32),
+            pltpu.SMEM(tags.shape, F32),
             pltpu.SemaphoreType.DMA((6 + 2 * CHUNKS,)),
             pltpu.SemaphoreType.DMA((n_i,)),
         ],
         compiler_params=pltpu.CompilerParams(vmem_limit_bytes=VMEM),
         name="product",
-    )(requests, slots, counts, rows, blocks, restrict, *got)
+    )(requests, slots, counts, rows, blocks, restrict, tags, *got)
 
 
 def reduce_kernel(g, acc_hbm, o_ref, acc, far, near, relay, relayed, s1, r2, sems, load, s2_send, s2_recv):
@@ -512,9 +524,9 @@
     restrict_rows,
 ):
     requests = fetch_lists.reshape(g.cols, g.slot).T
-    got = fetch(g, requests, prolong_cols.T, prolong_blocks)
+    tags, *got = fetch(g, requests, prolong_cols.T, prolong_blocks)
     acc = product(
-        g, requests, operator_slot, operator_count, restrict_rows.T, operator_blocks, restrict_blocks, got
+        g, requests, operator_slot, operator_count, restrict_rows.T, operator_blocks, restrict_blocks, tags, got
     )
     share = reduce(g, acc)
     return share.T

time: 116 us -> 115 us (level); the launches traced: 114 us -> 115 us
    pallas_call x1, Pallas kernels: 17.2 us -> 20.3 us  [reduce(): pl.pallas_call(functools.partial(reduce_kernel, g), out_shape=jax.ShapeDt...]
    pallas_call x1, Pallas kernels: 86.4 us -> 84 us  [fetch(): pl.pallas_call(functools.partial(fetch_kernel, g), out_shape=(jax.ShapeDt...]
where the time goes in v5:
time: 115 us
  Pallas kernels  113 us (98%)
  local copies, waits for them, and re-layouts  1.38 us (1%)
    pallas_call x1, Pallas kernels, fetch(): pl.pallas_call(functools.partial(fetch_kernel, g), out_shape=(jax.ShapeDt...  84 us
    pallas_call x1, Pallas kernels, reduce(): pl.pallas_call(functools.partial(reduce_kernel, g), out_shape=jax.ShapeDt...  20.3 us
    pallas_call x1, Pallas kernels, product(): pl.pallas_call(functools.partial(product_kernel, g, n_i, n_k), out_shape=...  8.87 us

profile of v5, /device:TPU:1, one launch (start us, length us, event | category | flops | bytes accessed | tf_op | source)
XLA Modules:
  0.0 114.6 jit_solution(17568243997153376088)
XLA Ops:
  0.0 84.0 %fetch.1 = (f32[32,1,128]{2,1,0:T(1,128)}, f32[32,64,128]{2,1,0:T(8,128)}, f32[32,64,128]{2,1,0:T(8,128)}, f32[64,32,128]{2,1,0:T(8,128)}, f32[64,32,128]{2,1,0:T(8,128)}) custom-call(s32[4,32]{1,0:T(4,128)} %bitcast.7, s32[2,8]{1,0:T(2,128)} %bitcast.9, f32[8,64,128]{2,1,0:T(8,128)} %p_hbm.1), custom_call_target="tpu_custom_call" | custom-call | tf_op jit(solution)/shard_map/fetch/pallas_call | solution.py:291
  84.1 8.9 %product.1.acc_hbm = f32[32,64,128]{2,1,0:T(8,128)} custom-call(s32[4,32]{1,0:T(4,128)} %bitcast.8, s32[8,8]{1,0:T(8,128)} %slot_hbm.1, s32[8]{0:T(128)} %count_hbm.1, s32[2,8]{1,0:T(2,128)} %bitcast.10, f32[8,64,512]{2,1,0:T(8,128)} %a_hbm.1, f32[8,64,128]{2,1,0:T(8,128)} %r_hbm.1, f32[32,1,128]{2,1,0:T(1,128)} %get-tuple-element.10.tag_hbm, ...), custom_call_target="tpu_custom_call" | custom-call | tf_op jit(solution)/shard_map/product/pallas_call | solution.py:401
  92.9 20.3 %reduce.1 = f32[64,128]{1,0:T(8,128)} custom-call(f32[32,64,128]{2,1,0:T(8,128)} %product.1.acc_hbm), custom_call_target="tpu_custom_call" | custom-call | tf_op jit(solution)/shard_map/reduce/pallas_call | solution.py:496
  113.2 1.4 %copy.10 = f32[128,64]{0,1:T(8,128)} copy(f32[128,64]{0,1:T(8,128)} %bitcast.6) | data formatting | bytes 65536
